TPU v7x, 256 devices: a whole 4x4x8 slice. The times are simulated.
256 devices in a mesh: dp: 2 (over core), context: 32 (over x, z), tensor: 4 (over y).
Axes of the slice: x: 4, y: 4, z: 8, core: 2. Of those that a mesh axis runs over, the one named last changes fastest.
Arguments:
- query_rows: bfloat16 [2, 8192, 4096], P('dp', 'context', 'tensor'), may hold values from -6 to 6
- key_rows: bfloat16 [2, 8192, 4096], P('dp', 'context', 'tensor'), may hold values from -6 to 6
- value_rows: bfloat16 [2, 8192, 4096], P('dp', 'context', 'tensor'), may hold values from -6 to 6
- filters: bfloat16 [256, 128], P('tensor'), may hold values from -0.5 to 0.5
- out_weight: bfloat16 [4096, 4096], P('tensor'), may hold values from -0.09375 to 0.09375
- lengths: int32 [2, 32], P('dp'), may hold values from 1 to 512, 8192 in all within a row
- panel_plan: int32 [2, 1024], P('dp'), may hold values from 0 to 1023, as said below
- out_grad: bfloat16 [2, 8192, 4096], P('dp', 'context', 'tensor'), may hold values from -6 to 6
Outputs:
- mixed: bfloat16 [2, 8192, 4096], P('dp', 'context', 'tensor')
- query_grad: bfloat16 [2, 8192, 4096], P('dp', 'context', 'tensor')
- key_grad: bfloat16 [2, 8192, 4096], P('dp', 'context', 'tensor')
- value_grad: bfloat16 [2, 8192, 4096], P('dp', 'context', 'tensor')
- filter_grad: float32 [256, 128], P('tensor')
Inputs may be any that keep to these rules, and one draw needn't show every extreme that they name: Each row of panel_plan is a permutation of 0 to 1023, and within each aligned block of 32 entries (the panels of one loader index of context) the values divided by 32, rounded down, are a permutation of 0 to 31. `lengths`: each row sums to 8192.
All inputs are finite; a program needn't handle non-finite values.
Results may differ from a plain program's by a relative error of at most 0.009.
Values may be sent and summed in bfloat16 or wider, within the bound.
A program may use at most 128 MiB of HBM per device.

v0:
```python
import math

import jax
import jax.numpy as jnp
from jax import lax
from jax.sharding import Mesh
from jax.sharding import PartitionSpec as P

CONTEXT = ("context_0", "context_1")
DP_CONTEXT = ("dp", "context_0", "context_1")


def sent_together(arrays, axis, split_dim, concat_dim, along):
    widths = [a.shape[along] for a in arrays]
    both = jnp.concatenate(arrays, axis=along)
    out = lax.all_to_all(both, axis, split_axis=split_dim, concat_axis=concat_dim, tiled=True)
    return tuple(jnp.split(out, [sum(widths[:k]) for k in range(1, len(widths))], axis=along))


def from_behind(value, axis, steps):
    count = lax.axis_size(axis)
    first, last = (max(0, -steps), min(count, count - steps))
    return lax.ppermute(value, axis, [(source, source + steps) for source in range(first, last)])


def in_blocks(shard, dim, length):
    before, after = (shard.shape[:dim], shard.shape[dim + 1 :])
    return jnp.moveaxis(shard.reshape(*before, length, -1, *after), dim, 0)


def summed_on_arrival(shard, axis, dim):
    blocks = in_blocks(shard, dim, lax.axis_size(axis))
    arrived = lax.all_to_all(blocks, axis, split_axis=0, concat_axis=0, tiled=True)
    return arrived.astype(jnp.float32).sum(axis=0)


def from_everyone(shard, axis):
    copies = jnp.broadcast_to(shard, (lax.axis_size(axis), *shard.shape))
    return lax.all_to_all(copies, axis, split_axis=0, concat_axis=0, tiled=True)


def laid_out(blocks, dim):
    shape = list(blocks.shape[1:])
    shape[dim] *= blocks.shape[0]
    return jnp.moveaxis(blocks, 0, dim).reshape(shape)


def collect(shard, axis, dim):
    blocks = from_everyone(shard, axis)
    return laid_out(blocks, dim)


def over_axes(shard, axes):
    for axis in axes:
        shard = lax.psum(shard, axis)
    return shard


def regroup(matrix, rows_in):
    count = matrix.shape[1]
    flat = rows_in.reshape(count, -1)
    moved = jnp.dot(matrix, flat, preferred_element_type=jnp.float32)
    return moved.astype(jnp.bfloat16).reshape(rows_in.shape)


def doc_ages(positions, lengths_row):
    starts = jnp.cumsum(lengths_row) - lengths_row
    begin = jnp.max(jnp.where(starts[None, :] <= positions[:, None], starts[None, :], 0), axis=1)
    return positions - begin


def band_matrix(filters, tap_table):
    groups, taps = filters.shape
    flat = jnp.dot(filters, tap_table.reshape(taps, -1), preferred_element_type=jnp.float32)
    return flat.astype(jnp.bfloat16).reshape(groups, 2 * taps, taps)


def time_major(rows, groups, taps):
    total, width = rows.shape
    columns = rows.T.reshape(groups, width // groups, total)
    head = columns[:, :, : total - taps].reshape(groups, width // groups, -1, taps)
    tail = columns[:, :, taps:].reshape(groups, width // groups, -1, taps)
    return (head, tail)


def per_device(
    query_rows, key_rows, value_rows, filters, out_weight, lengths, panel_plan, out_grad
):
    groups, taps = filters.shape
    length, width = (query_rows.shape[1], query_rows.shape[2])
    block_count = length // taps
    panel_count = lax.axis_size(CONTEXT)
    device_rank = lax.axis_index(CONTEXT)
    plan_rows = panel_plan[0].reshape(panel_count, panel_count)
    own_plan = lax.dynamic_slice_in_dim(plan_rows, device_rank, 1, 0)[0]
    slot_ids = jnp.arange(panel_count, dtype=jnp.int32)
    select = (own_plan[None, :] // panel_count == slot_ids[:, None]).astype(jnp.bfloat16)
    sender_slot = jnp.sum(
        jnp.where(plan_rows // panel_count == device_rank, plan_rows % panel_count, 0), axis=1
    )
    placing = (sender_slot[None, :] == slot_ids[:, None]).astype(jnp.bfloat16)
    local_product = (key_rows[0].astype(jnp.float32) * value_rows[0].astype(jnp.float32)).astype(
        jnp.bfloat16
    )
    arrived = sent_together(
        (regroup(select, query_rows[0]), regroup(select, local_product)), CONTEXT, 0, 0, 1
    )
    query_own = regroup(placing, arrived[0])
    product = regroup(placing, arrived[1])
    tap_ids = jnp.arange(taps, dtype=jnp.int32)
    out_ids = jnp.arange(taps, dtype=jnp.int32)
    win_ids = jnp.arange(2 * taps, dtype=jnp.int32)
    fwd_lag = out_ids[None, :] + taps - win_ids[:, None]
    bwd_lag = win_ids[:, None] - out_ids[None, :]
    fwd_table = (fwd_lag[None] == tap_ids[:, None, None]).astype(jnp.bfloat16)
    bwd_table = (bwd_lag[None] == tap_ids[:, None, None]).astype(jnp.bfloat16)
    fwd_band = band_matrix(filters, fwd_table)
    bwd_band = band_matrix(filters, bwd_table)
    positions = device_rank * length + jnp.arange(length + taps, dtype=jnp.int32)
    age_all = doc_ages(positions, lengths[0])
    age_here = age_all[:length].reshape(block_count, taps)
    age_windows = jnp.concatenate(
        [age_all[:length].reshape(block_count, taps), age_all[taps:].reshape(block_count, taps)],
        axis=1,
    )
    fwd_mask = fwd_lag[None] <= age_here[:, None, :]
    bwd_mask = bwd_lag[None] <= age_windows[:, :, None]
    rim_rows = from_behind(product[length - taps + 1 :], CONTEXT, 1)
    padded = jnp.concatenate([jnp.zeros((1, width), jnp.bfloat16), rim_rows, product], axis=0)
    prod_head, prod_tail = time_major(padded, groups, taps)
    masked = fwd_band[None] * fwd_mask[:, None].astype(jnp.bfloat16)
    conv_cols = jnp.einsum(
        "gcks,kgst->gckt", prod_head, masked[:, :, :taps], preferred_element_type=jnp.float32
    )
    conv_cols = conv_cols + jnp.einsum(
        "gcks,kgst->gckt", prod_tail, masked[:, :, taps:], preferred_element_type=jnp.float32
    )
    conv = conv_cols.reshape(width, length).T
    gated = (query_own.astype(jnp.float32) * conv).astype(jnp.bfloat16)
    partial_value = jnp.dot(gated, out_weight, preferred_element_type=jnp.float32)
    mixed = summed_on_arrival(partial_value.astype(jnp.bfloat16), "tensor", 1).astype(jnp.bfloat16)[
        None
    ]
    grad_gated = lax.dot_general(
        collect(out_grad[0], "tensor", 1),
        out_weight,
        (((1,), (1,)), ((), ())),
        preferred_element_type=jnp.float32,
    )
    query_back = (grad_gated * conv).astype(jnp.bfloat16)
    conv_back = (grad_gated * query_own.astype(jnp.float32)).astype(jnp.bfloat16)
    rim_back = from_behind(conv_back[: taps - 1], CONTEXT, -1)
    padded_back = jnp.concatenate(
        [conv_back, rim_back, jnp.zeros((1, width), jnp.bfloat16)], axis=0
    )
    back_head, back_tail = time_major(padded_back, groups, taps)
    back_masked = bwd_band[None] * bwd_mask[:, None].astype(jnp.bfloat16)
    back_cols = jnp.einsum(
        "gckt,kgts->gcks", back_head, back_masked[:, :, :taps], preferred_element_type=jnp.float32
    )
    back_cols = back_cols + jnp.einsum(
        "gckt,kgts->gcks", back_tail, back_masked[:, :, taps:], preferred_element_type=jnp.float32
    )
    product_back = back_cols.reshape(width, length).T.astype(jnp.bfloat16)
    mask_float = fwd_mask.astype(jnp.float32)
    outer_head = jnp.einsum(
        "gcks,gckt->kgst", prod_head, back_head, preferred_element_type=jnp.float32
    )
    outer_tail = jnp.einsum(
        "gcks,gckt->kgst", prod_tail, back_head, preferred_element_type=jnp.float32
    )
    summed_head = jnp.sum(outer_head * mask_float[:, None, :taps], axis=0).reshape(
        groups, taps * taps
    )
    summed_tail = jnp.sum(outer_tail * mask_float[:, None, taps:], axis=0).reshape(
        groups, taps * taps
    )
    table_float = fwd_table.astype(jnp.float32)
    table_head = table_float[:, :taps].reshape(taps, taps * taps)
    table_tail = table_float[:, taps:].reshape(taps, taps * taps)
    dims = (((1,), (1,)), ((), ()))
    tap_sums = lax.dot_general(
        summed_head,
        table_head,
        dims,
        precision=lax.Precision.HIGHEST,
        preferred_element_type=jnp.float32,
    )
    tap_sums = tap_sums + lax.dot_general(
        summed_tail,
        table_tail,
        dims,
        precision=lax.Precision.HIGHEST,
        preferred_element_type=jnp.float32,
    )
    total_tokens = lax.axis_size("dp") * panel_count * length
    scale = 1.0 / math.sqrt(float(total_tokens))
    filter_grad = over_axes(tap_sums * scale, DP_CONTEXT)
    back_placing = placing.T
    back_select = select.T
    returned = sent_together(
        (regroup(back_placing, query_back), regroup(back_placing, product_back)), CONTEXT, 0, 0, 1
    )
    query_grad = regroup(back_select, returned[0])
    product_home = regroup(back_select, returned[1]).astype(jnp.float32)
    key_grad = (product_home * value_rows[0].astype(jnp.float32)).astype(jnp.bfloat16)
    value_grad = (product_home * key_rows[0].astype(jnp.float32)).astype(jnp.bfloat16)
    return (mixed, query_grad[None], key_grad[None], value_grad[None], filter_grad)


def solution(mesh):
    finer = Mesh(
        mesh.devices.reshape(mesh.shape["dp"], 4, 8, mesh.shape["tensor"]),
        ("dp", "context_0", "context_1", "tensor"),
    )
    in_specs = (
        P("dp", CONTEXT, "tensor"),
        P("dp", CONTEXT, "tensor"),
        P("dp", CONTEXT, "tensor"),
        P("tensor", None),
        P("tensor", None),
        P("dp", None),
        P("dp", None),
        P("dp", CONTEXT, "tensor"),
    )
    out_specs = (
        P("dp", CONTEXT, "tensor"),
        P("dp", CONTEXT, "tensor"),
        P("dp", CONTEXT, "tensor"),
        P("dp", CONTEXT, "tensor"),
        P("tensor", None),
    )
    return jax.shard_map(
        per_device, mesh=finer, in_specs=in_specs, out_specs=out_specs, check_vma=False
    )
```

profile of v0, /device:TPU:8, one launch (start us, length us, event | category | flops | bytes accessed | tf_op | source)
XLA Modules:
  0.0 220.8 jit_solution(11974155271854987153)
XLA Ops:
  6.8 12.0 %all-to-all-start = ((bf16[32,8,2048]{2,1,0:T(8,128)(2,1)}), bf16[32,8,2048]{2,1,0:T(8,128)(2,1)}, u32[]{:S(2)}, u32[]{:S(2)}) async-start(bf16[32,8,2048]{2,1,0:T(8,128)(2,1)} %pad_maximum_fusion), calls=%async_computation | async-start | bytes 2097152 | tf_op jit(solution)/shard_map/all_to_all | solution.py:16
  20.0 3.9 %fusion.18 = bf16[8,8,256,128]{3,1,2,0:T(8,128)(2,1)S(1)} fusion(bf16[64,128]{1,0:T(8,128)(2,1)S(1)} %copy-done, s32[32768]{0:T(1024)S(1)} %get-tuple-element.23), kind=kOutput, calls=%fused_computation.36 | convolution fusion | flops 543162368 | bytes 4341760 | tf_op jit(solution)/shard_map/dot_general | solution.py:74
  24.7 5.9 %fusion.19 = bf16[8,8,256,128]{3,1,2,0:T(8,128)(2,1)} fusion(bf16[64,128]{1,0:T(8,128)(2,1)S(1)} %copy-done, s32[32768]{0:T(1024)S(1)} %fusion.77), kind=kOutput, calls=%fused_computation.37 | convolution fusion | flops 543162368 | bytes 4341760 | tf_op jit(solution)/shard_map/dot_general | solution.py:74
  31.7 3.1 %copy.95 = bf16[8,8,256,128]{3,2,1,0:T(8,128)(2,1)} copy(bf16[8,8,256,128]{3,1,2,0:T(8,128)(2,1)S(1)} %fusion.18) | data formatting | bytes 8388608
  35.1 5.4 %copy.98 = bf16[8,8,256,128]{3,2,1,0:T(8,128)(2,1)} copy(bf16[8,8,256,128]{3,1,2,0:T(8,128)(2,1)} %fusion.19) | data formatting | bytes 8388608
  40.6 4.7 %broadcast_multiply_fusion.1 = bf16[2,64,256,128]{3,2,0,1:T(8,128)(2,1)} fusion(bf16[2,256,128]{2,1,0:T(8,128)(2,1)} %get-tuple-element.20, bf16[64,256,128]{2,1,0:T(8,128)(2,1)S(1)} %bitcast.132), kind=kLoop, calls=%fused_computation.35 | loop fusion | flops 4194304 | bytes 12713984 | tf_op jit(solution)/shard_map/mul | solution.py:131
  45.3 6.0 %broadcast_multiply_fusion = bf16[2,64,256,128]{3,2,0,1:T(8,128)(2,1)} fusion(bf16[2,256,128]{2,1,0:T(8,128)(2,1)} %compare_convert_fusion.2, bf16[64,256,128]{2,1,0:T(8,128)(2,1)} %bitcast.133), kind=kLoop, calls=%fused_computation.34 | loop fusion | flops 4194304 | bytes 12713984 | tf_op jit(solution)/shard_map/mul | solution.py:157
  52.8 4.9 %all-to-all-start.2 = ((bf16[4,256,1024]{1,2,0:T(8,128)(2,1)}), bf16[4,256,1024]{1,2,0:T(8,128)(2,1)}, u32[]{:S(2)}, u32[]{:S(2)}) async-start(bf16[4,256,1024]{1,2,0:T(8,128)(2,1)} %broadcast_in_dim.14), calls=%async_computation.2 | async-start | bytes 4194304 | tf_op jit(solution)/shard_map/all_to_all | solution.py:39
  60.2 4.0 %collective-permute-start = (bf16[127,1024]{0,1:T(8,128)(2,1)S(1)}, bf16[127,1024]{0,1:T(8,128)(2,1)S(1)}, u32[]{:S(2)}, u32[]{:S(2)}) collective-permute-start(bf16[127,1024]{0,1:T(8,128)(2,1)S(1)} %slice.71), channel_id=1, source_target_pairs={{0,4},{4,8},{8,12},{12,16},{16,20},{20,24},{24,28},{28,32},{32,36}... | collective-permute-start | bytes 780296 | tf_op jit(solution)/shard_map/ppermute | solution.py:23
  65.6 3.1 %collective-permute-done = bf16[127,1024]{0,1:T(8,128)(2,1)S(1)} collective-permute-done((bf16[127,1024]{0,1:T(8,128)(2,1)S(1)}, bf16[127,1024]{0,1:T(8,128)(2,1)S(1)}, u32[]{:S(2)}, u32[]{:S(2)}) %collective-permute-start) | collective-permute-done | bytes 260128 | tf_op jit(solution)/shard_map/ppermute | solution.py:23
  69.9 3.4 %fusion.12 = f32[64,2,128,16]{2,3,1,0:T(8,128)S(1)} fusion(bf16[2,64,256,128]{3,2,0,1:T(8,128)(2,1)} %broadcast_multiply_fusion.1, bf16[64,2,2,8,128]{4,3,2,1,0:T(8,128)(2,1)S(1)} %get-tuple-element.16), kind=kOutput, calls=%fused_computation.28 | convolution fusion | flops 67108864 | bytes 5767168 | tf_op jit(solution)/shard_map/gcks,kgst->gckt/dot_general | solution.py:135
  73.3 3.4 %fusion.23 = f32[64,16,2,128]{3,1,2,0:T(8,128)S(1)} fusion(f32[64,2,128,16]{2,3,1,0:T(8,128)S(1)} %fusion.12, bf16[2,64,256,128]{3,2,0,1:T(8,128)(2,1)} %broadcast_multiply_fusion.1, bf16[64,2,2,8,128]{4,3,2,1,0:T(8,128)(2,1)S(1)} %get-tuple-element.15), kind=kOutput, calls=%fused_computation.40 | convolution fusion | flops 67371008 | bytes 6815744 | tf_op jit(solution)/shard_map/gcks,kgst->gckt/dot_general | solution.py:132
  78.8 3.9 %all-to-all-done.2 = bf16[4,256,1024]{1,2,0:T(8,128)(2,1)} async-done(((bf16[4,256,1024]{1,2,0:T(8,128)(2,1)}), bf16[4,256,1024]{1,2,0:T(8,128)(2,1)}, u32[]{:S(2)}, u32[]{:S(2)}) %all-to-all-start.2) | async-done | bytes 2097184 | tf_op jit(solution)/shard_map/all_to_all | solution.py:39
  82.7 7.5 %fusion.59 = (bf16[256,1024]{1,0:T(8,128)(2,1)}, bf16[256,1024]{1,0:T(8,128)(2,1)S(1)}) fusion(f32[1024,256]{0,1:T(8,128)} %copy.70, f32[256,1024]{1,0:T(8,128)S(1)} %reshape.225, bf16[256,4096]{0,1:T(8,128)(2,1)} %bitcast.16, bf16[1024,4096]{1,0:T(8,128)(2,1)} %param.12), kind=kOutput, calls=%fused_computation.60 | convolution fusion | flops 2148532224 | bytes 13631488 | tf_op jit(solution)/shard_map/dot_general | solution.py:144
  92.5 6.1 %convolution_convert_fusion.10 = bf16[256,4096]{1,0:T(8,128)(2,1)S(1)} fusion(bf16[1024,4096]{1,0:T(8,128)(2,1)} %param.12, f32[256,1024]{1,0:T(8,128)} %copy-done.9, f32[1024,256]{0,1:T(8,128)S(1)} %copy-done.10), kind=kOutput, calls=%fused_computation.23 | convolution fusion | flops 2149056512 | bytes 12582912 | tf_op jit(solution)/shard_map/dot_general | solution.py:140
  102.9 5.0 %all-to-all-start.1 = ((bf16[4,256,1024]{2,1,0:T(8,128)(2,1)}), bf16[4,256,1024]{2,1,0:T(8,128)(2,1)S(1)}, u32[]{:S(2)}, u32[]{:S(2)}) async-start(bf16[4,256,1024]{2,1,0:T(8,128)(2,1)} %bitcast.134), calls=%async_computation.1 | async-start | bytes 4194304 | tf_op jit(solution)/shard_map/all_to_all | solution.py:33
  107.9 2.0 maximum_bitcast_fusion
  109.9 2.3 %copy.73 = bf16[1024,384]{1,0:T(8,128)(2,1)} copy(bf16[1024,384]{0,1:T(8,128)(2,1)} %maximum_bitcast_fusion) | data formatting | bytes 1572864 | tf_op jit(solution)/shard_map/transpose | solution.py:80
  113.5 3.4 %fusion.8 = f32[64,2,128,16]{2,3,1,0:T(8,128)S(1)} fusion(bf16[2,64,256,128]{3,2,0,1:T(8,128)(2,1)} %broadcast_multiply_fusion, bf16[64,2,2,8,128]{4,3,2,1,0:T(8,128)(2,1)S(1)} %get-tuple-element.14), kind=kOutput, calls=%fused_computation.24 | convolution fusion | flops 67108864 | bytes 5767168 | tf_op jit(solution)/shard_map/gckt,kgts->gcks/dot_general | solution.py:161
  117.0 3.4 %fusion.32 = bf16[64,16,2,128]{3,1,2,0:T(8,128)(2,1)S(1)} fusion(f32[64,2,128,16]{2,3,1,0:T(8,128)S(1)} %fusion.8, bf16[2,64,256,128]{3,2,0,1:T(8,128)(2,1)} %broadcast_multiply_fusion, bf16[64,2,2,8,128]{4,3,2,1,0:T(8,128)(2,1)S(1)} %get-tuple-element.13), kind=kOutput, calls=%fused_computation.46 | convolution fusion | flops 67633152 | bytes 6291456 | tf_op jit(solution)/shard_map/gckt,kgts->gcks/dot_general | solution.py:158
  121.7 2.0 copy.77
  123.7 2.1 reshape.222
  127.5 2.1 pad_maximum_fusion.1
  129.6 2.3 %all-to-all-done.1 = bf16[4,256,1024]{2,1,0:T(8,128)(2,1)S(1)} async-done(((bf16[4,256,1024]{2,1,0:T(8,128)(2,1)}), bf16[4,256,1024]{2,1,0:T(8,128)(2,1)S(1)}, u32[]{:S(2)}, u32[]{:S(2)}) %all-to-all-start.1) | async-done | bytes 2097184 | tf_op jit(solution)/shard_map/all_to_all | solution.py:33
  131.8 10.6 %all-to-all-start.3 = ((bf16[32,8,2048]{2,1,0:T(8,128)(2,1)}), bf16[32,8,2048]{2,1,0:T(8,128)(2,1)}, u32[]{:S(2)}, u32[]{:S(2)}) async-start(bf16[32,8,2048]{2,1,0:T(8,128)(2,1)} %pad_maximum_fusion.1), calls=%async_computation.3 | async-start | bytes 2097152 | tf_op jit(solution)/shard_map/all_to_all | solution.py:16
  142.5 2.7 %iota_compare_fusion = pred[128,256,128]{2,0,1:T(32,128)(4,1)S(1)} fusion(s32[256,128]{1,0:T(8,128)S(1)} %get-tuple-element.24), kind=kLoop, calls=%fused_computation.2 | loop fusion | flops 4194304 | bytes 4325376 | tf_op jit(solution)/shard_map/eq | solution.py:115
  148.2 6.4 %fusion.35 = f32[64,128]{1,0:T(8,128)S(1)} fusion(pred[128,256,128]{2,0,1:T(32,128)(4,1)S(1)} %iota_compare_fusion, f32[64,128,128]{2,1,0:T(8,128)S(1)} %multiply_reduce_fusion.1), kind=kOutput, calls=%fused_computation.47 | convolution fusion | flops 1610612736 | bytes 6324224 | tf_op jit(solution)/shard_map/dot_general | solution.py:182
  154.6 6.8 %fusion.50 = f32[64,128]{1,0:T(8,128)S(1)} fusion(f32[64,128]{1,0:T(8,128)S(1)} %fusion.35, pred[128,256,128]{2,0,1:T(32,128)(4,1)S(1)} %iota_compare_fusion, f32[64,128,128]{2,1,0:T(8,128)S(1)} %multiply_reduce_fusion), kind=kOutput, calls=%fused_computation.50 | convolution fusion | flops 1610629120 | bytes 6356992 | tf_op jit(solution)/shard_map/dot_general | solution.py:189
  161.4 3.4 %psum.21 = f32[64,128]{1,0:T(8,128)S(1)} all-reduce(f32[64,128]{1,0:T(8,128)S(1)} %fusion.50), channel_id=1, replica_groups=mesh['dp'=2,'context_0'=4,'context_1'=8,'tensor'=4] {'dp'}, use_global_device_ids=true, to_apply=%region_6.7 | all-reduce | flops 8192 | bytes 65536 | tf_op jit(solution)/shard_map/psum | solution.py:55
  164.8 17.3 %psum.22 = f32[64,128]{1,0:T(8,128)S(1)} all-reduce(f32[64,128]{1,0:T(8,128)S(1)} %psum.21), channel_id=1, replica_groups=mesh['dp'=2,'context_0'=4,'context_1'=8,'tensor'=4] {'context_0'}, use_global_device_ids=true, to_apply=%region_7.8 | all-reduce | flops 8192 | bytes 65536 | tf_op jit(solution)/shard_map/psum | solution.py:55
  182.1 30.2 %psum.23 = f32[64,128]{1,0:T(8,128)} all-reduce(f32[64,128]{1,0:T(8,128)S(1)} %psum.22), channel_id=1, replica_groups=mesh['dp'=2,'context_0'=4,'context_1'=8,'tensor'=4] {'context_1'}, use_global_device_ids=true, to_apply=%region_8.9 | all-reduce | flops 8192 | bytes 65536 | tf_op jit(solution)/shard_map/psum | solution.py:55
  213.7 2.1 fusion.93
  (115 shorter events, 37.9 us)
Async XLA Ops:
  0.6 19.3 %copy-start = (bf16[64,128]{1,0:T(8,128)(2,1)S(1)}, bf16[64,128]{1,0:T(8,128)(2,1)}, u32[]{:S(2)}) copy-start(bf16[64,128]{1,0:T(8,128)(2,1)} %param.11) | copy-start | bytes 49156
  0.6 4.2 %copy-start.11 = (bf16[1,256,1024]{2,1,0:T(8,128)(2,1)S(1)}, bf16[1,256,1024]{2,1,0:T(8,128)(2,1)}, u32[]{:S(2)}) copy-start(bf16[1,256,1024]{2,1,0:T(8,128)(2,1)} %param.8) | copy-start | bytes 1572868
  2.6 4.2 %copy-start.13 = (s32[32,32]{1,0:T(8,128)}, s32[32,32]{1,0:T(8,128)S(1)}, u32[]{:S(2)}) copy-start(s32[32,32]{1,0:T(8,128)S(1)} %reshape_squeeze.6) | copy-start | bytes 12292
  4.3 2.5 %copy-start.17 = (s32[32]{0:T(128)}, s32[32]{0:T(128)S(1)}, u32[]{:S(2)}) copy-start(s32[32]{0:T(128)S(1)} %fusion.92) | copy-start | bytes 388
  4.6 14.2 %copy-start.21 = (s32[1,32]{1,0:T(1,128)S(1)}, s32[1,32]{1,0:T(1,128)}, u32[]{:S(2)}) copy-start(s32[1,32]{1,0:T(1,128)} %param.13) | copy-start | bytes 388
  6.8 44.5 %all-to-all-start = ((bf16[32,8,2048]{2,1,0:T(8,128)(2,1)}), bf16[32,8,2048]{2,1,0:T(8,128)(2,1)}, u32[]{:S(2)}, u32[]{:S(2)}) async-start(bf16[32,8,2048]{2,1,0:T(8,128)(2,1)} %pad_maximum_fusion), calls=%async_computation | async-start | bytes 2097152 | tf_op jit(solution)/shard_map/all_to_all | solution.py:16
  31.7 3.1 %copy-start.12 = (bf16[1,256,1024]{2,1,0:T(8,128)(2,1)S(1)}, bf16[1,256,1024]{2,1,0:T(8,128)(2,1)}, u32[]{:S(2)}) copy-start(bf16[1,256,1024]{2,1,0:T(8,128)(2,1)} %param.15) | copy-start | bytes 1572868
  35.0 5.5 %copy-start.14 = (s32[32,32]{1,0:T(8,128)S(1)}, s32[32,32]{1,0:T(8,128)}, u32[]{:S(2)}) copy-start(s32[32,32]{1,0:T(8,128)} %copy-done.13) | copy-start | bytes 12292
  35.0 5.6 %copy-start.2 = (bf16[8,8,256,128]{3,2,1,0:T(8,128)(2,1)S(1)}, bf16[8,8,256,128]{3,2,1,0:T(8,128)(2,1)}, u32[]{:S(2)}) copy-start(bf16[8,8,256,128]{3,2,1,0:T(8,128)(2,1)} %copy.95) | copy-start | bytes 12582916
  40.6 18.6 %copy-start.15 = (s32[32]{0:T(128)}, s32[32]{0:T(128)S(1)}, u32[]{:S(2)}) copy-start(s32[32]{0:T(128)S(1)} %fusion.81) | copy-start | bytes 388
  52.8 29.9 %all-to-all-start.2 = ((bf16[4,256,1024]{1,2,0:T(8,128)(2,1)}), bf16[4,256,1024]{1,2,0:T(8,128)(2,1)}, u32[]{:S(2)}, u32[]{:S(2)}) async-start(bf16[4,256,1024]{1,2,0:T(8,128)(2,1)} %broadcast_in_dim.14), calls=%async_computation.2 | async-start | bytes 4194304 | tf_op jit(solution)/shard_map/all_to_all | solution.py:39
  59.3 9.4 %copy-start.20 = (bf16[384]{0:T(512)(128)(2,1)S(1)}, bf16[384]{0:T(512)(128)(2,1)}, u32[]{:S(2)}) copy-start(bf16[384]{0:T(512)(128)(2,1)} %pad.7.clone) | copy-start | bytes 2308
  60.2 8.5 %collective-permute-start = (bf16[127,1024]{0,1:T(8,128)(2,1)S(1)}, bf16[127,1024]{0,1:T(8,128)(2,1)S(1)}, u32[]{:S(2)}, u32[]{:S(2)}) collective-permute-start(bf16[127,1024]{0,1:T(8,128)(2,1)S(1)} %slice.71), channel_id=1, source_target_pairs={{0,4},{4,8},{8,12},{12,16},{16,20},{20,24},{24,28},{28,32},{32,36}... | collective-permute-start | bytes 780296 | tf_op jit(solution)/shard_map/ppermute | solution.py:23
  65.5 17.2 %copy-start.9 = (f32[256,1024]{1,0:T(8,128)}, f32[256,1024]{1,0:T(8,128)S(1)}, u32[]{:S(2)}) copy-start(f32[256,1024]{1,0:T(8,128)S(1)} %reshape.225) | copy-start | bytes 3145732
  69.1 0.8 copy-start.3
  82.7 9.7 %copy-start.10 = (f32[1024,256]{0,1:T(8,128)S(1)}, f32[1024,256]{0,1:T(8,128)}, u32[]{:S(2)}) copy-start(f32[1024,256]{0,1:T(8,128)} %copy.70) | copy-start | bytes 3145732
  90.2 8.3 %copy-start.7 = (bf16[256,1024]{1,0:T(8,128)(2,1)}, bf16[256,1024]{1,0:T(8,128)(2,1)S(1)}, u32[]{:S(2)}) copy-start(bf16[256,1024]{1,0:T(8,128)(2,1)S(1)} %get-tuple-element.10) | copy-start | bytes 1572868
  91.0 8.8 %copy-start.16 = (s32[32]{0:T(128)S(1)}, s32[32]{0:T(128)}, u32[]{:S(2)}) copy-start(s32[32]{0:T(128)} %copy-done.15) | copy-start | bytes 388
  91.0 16.8 %collective-permute-start.1 = (bf16[127,1024]{1,0:T(8,128)(2,1)}, bf16[127,1024]{1,0:T(8,128)(2,1)}, u32[]{:S(2)}, u32[]{:S(2)}) collective-permute-start(bf16[127,1024]{1,0:T(8,128)(2,1)} %slice.76), channel_id=1, source_target_pairs={{4,0},{8,4},{12,8},{16,12},{20,16},{24,20},{28,24},{32,28},{36,32}... | collective-permute-start | bytes 780296 | tf_op jit(solution)/shard_map/ppermute | solution.py:23
  101.3 6.6 %copy-start.8 = (bf16[256,1024]{1,0:T(8,128)(2,1)S(1)}, bf16[256,1024]{1,0:T(8,128)(2,1)}, u32[]{:S(2)}) copy-start(bf16[256,1024]{1,0:T(8,128)(2,1)} %copy-done.7) | copy-start | bytes 1572868
  101.3 6.6 %copy-start.19 = (bf16[384]{0:T(512)(128)(2,1)S(1)}, bf16[384]{0:T(512)(128)(2,1)}, u32[]{:S(2)}) copy-start(bf16[384]{0:T(512)(128)(2,1)} %pad.6.clone) | copy-start | bytes 2308
  102.9 28.9 %all-to-all-start.1 = ((bf16[4,256,1024]{2,1,0:T(8,128)(2,1)}), bf16[4,256,1024]{2,1,0:T(8,128)(2,1)S(1)}, u32[]{:S(2)}, u32[]{:S(2)}) async-start(bf16[4,256,1024]{2,1,0:T(8,128)(2,1)} %bitcast.134), calls=%async_computation.1 | async-start | bytes 4194304 | tf_op jit(solution)/shard_map/all_to_all | solution.py:33
  131.8 81.8 %all-to-all-start.3 = ((bf16[32,8,2048]{2,1,0:T(8,128)(2,1)}), bf16[32,8,2048]{2,1,0:T(8,128)(2,1)}, u32[]{:S(2)}, u32[]{:S(2)}) async-start(bf16[32,8,2048]{2,1,0:T(8,128)(2,1)} %pad_maximum_fusion.1), calls=%async_computation.3 | async-start | bytes 2097152 | tf_op jit(solution)/shard_map/all_to_all | solution.py:16
  142.4 2.7 %copy-start.4 = (bf16[64,2,2,8,128]{4,3,2,1,0:T(8,128)(2,1)S(1)}, bf16[64,2,2,8,128]{4,3,2,1,0:T(8,128)(2,1)}, u32[]{:S(2)}) copy-start(bf16[64,2,2,8,128]{4,3,2,1,0:T(8,128)(2,1)} %copy-done.3) | copy-start | bytes 1572868
  161.4 54.6 %copy-start.18 = (s32[32]{0:T(128)S(1)}, s32[32]{0:T(128)}, u32[]{:S(2)}) copy-start(s32[32]{0:T(128)} %copy-done.17) | copy-start | bytes 388
  212.3 4.2 %copy-start.5 = (bf16[1,256,1024]{2,1,0:T(8,128)(2,1)S(1)}, bf16[1,256,1024]{2,1,0:T(8,128)(2,1)}, u32[]{:S(2)}) copy-start(bf16[1,256,1024]{2,1,0:T(8,128)(2,1)} %param.10) | copy-start | bytes 1572868
  212.3 4.2 %copy-start.6 = (bf16[1,256,1024]{2,1,0:T(8,128)(2,1)S(1)}, bf16[1,256,1024]{2,1,0:T(8,128)(2,1)}, u32[]{:S(2)}) copy-start(bf16[1,256,1024]{2,1,0:T(8,128)(2,1)} %param.9) | copy-start | bytes 1572868
  216.0 4.5 %copy-start.1 = (bf16[64,128]{1,0:T(8,128)(2,1)S(1)}, bf16[64,128]{1,0:T(8,128)(2,1)}, u32[]{:S(2)}) copy-start(bf16[64,128]{1,0:T(8,128)(2,1)} %param.11) | copy-start | bytes 49156
where the time goes:
time: 224 us; the launch traced here: 221 us
  matrix products  57.4 us (26%)
  blocking collectives  50.9 us (23%)
  starting transfers between devices  37.8 us (17%)
  local copies, waits for them, and re-layouts  37.6 us (17%)
  other arithmetic  26.2 us (12%)
  waiting for transfers between devices  9.28 us (4%)
    psum x3, blocking collectives, over_axes(): shard = lax.psum(shard, axis)  50.9 us
    all_to_all x2, starting transfers between devices, sent_together(): lax.all_to_all(both, axis, split_axis=split_dim, concat_axis=concat_dim,...  22.6 us
    unnamed x55, local copies, waits for them, and re-layouts  14.4 us
    dot_general x2, matrix products, band_matrix(): jnp.dot(filters, tap_table.reshape(taps, -1), preferred_element_type=jnp....  9.74 us
    dot_general x1, matrix products, per_device(): lax.dot_general(collect(out_grad[0], 'tensor', 1), out_weight, (((1,), (1...  7.49 us
    dot_general x1, matrix products, per_device(): lax.dot_general(summed_tail, table_tail, dims, precision=lax.Precision.HI...  6.78 us
    dot_general x1, matrix products, per_device(): lax.dot_general(summed_head, table_head, dims, precision=lax.Precision.HI...  6.4 us
    dot_general x1, matrix products, per_device(): jnp.dot(gated, out_weight, preferred_element_type=jnp.float32)  6.09 us
  transfers between devices with their start and end apart: 6, of which 3 were waited for; matrix products, arithmetic and copies ran while one was open for 44% of the time, Pallas kernels for 0%

commit v1 on v0

v1 whole, which is shorter than its diff:
```python
import functools
import math

import jax
import jax.numpy as jnp
from jax import lax
from jax.experimental import pallas as pl
from jax.experimental.pallas import tpu as pltpu
from jax.sharding import Mesh
from jax.sharding import PartitionSpec as P

DP, CX, CZ, TP = "dp", "context_0", "context_1", "tensor"
CONTEXT = (CX, CZ)
BF = jnp.bfloat16
F32 = jnp.float32
I32 = jnp.int32
LANES = 128
CHUNKS = 4
MESH_ID = pl.DeviceIdType.MESH
NT = (((1,), (1,)), ((), ()))


def log2(n):
    return n.bit_length() - 1


def iota(shape, dim):
    return lax.broadcasted_iota(I32, shape, dim)


def ones_where(cond):
    return jnp.where(cond, 1.0, 0.0)


def mm(a, b):
    return jnp.dot(a, b, preferred_element_type=F32)


def mm_nt(a, b):
    return lax.dot_general(a, b, NT, preferred_element_type=F32)


def layer_kernel(
    cfg,
    plan_s, len_s, plan_v, filt_v, q_hbm, k_hbm, v_hbm, og_hbm, w_hbm,
    mixed_o, qg_o, kg_o, vg_o, fg_o,
    x1, kv, vv, w, og, fmat, hmat, pmat, rmat, sbuf, rbuf, sbuf2, rbuf2,
    qo, pw, cbw, x2, gated, gg, acc, tf, tb, mf, mb, mflip,
    rs_send, rs_recv, tap, tap1, tap2, tap3,
    ld, fs, fr, ags, agr, phs, phr, chs, chr_, bs, br, rss, rsr, t1s, t1r, t2s, t2r, t3s, t3r,
):
    n, nx, nz, ny, ndp = cfg["n"], cfg["nx"], cfg["nz"], cfg["ny"], cfg["ndp"]
    length, width, taps, docs = cfg["length"], cfg["width"], cfg["taps"], cfg["docs"]
    psz, gsz, total = length // n, 16, length * n
    cw = width // CHUNKS
    cols = cw // LANES
    blocks = length // taps
    per = LANES // gsz
    rows = per * taps
    lgn, lgp = log2(n), log2(psz)

    dp, cx, cz, ty = (lax.axis_index(a) for a in (DP, CX, CZ, TP))
    me = cx * nz + cz
    group_n = ndp * nx
    e_me = dp * nx + cx

    def ctx(index):
        return {CX: index // nz, CZ: lax.rem(index, nz)}

    def peer_e(index):
        return {DP: index // nx, CX: lax.rem(index, nx)}

    def after(k):
        return lax.rem(me + k, n)

    loads = [
        pltpu.make_async_copy(src, dst, ld.at[i])
        for i, (src, dst) in enumerate(
            [
                (k_hbm, kv),
                (v_hbm, vv),
                (q_hbm, x1.at[pl.ds(0, length)]),
                (og_hbm, og.at[ty]),
                (w_hbm, w),
            ]
        )
    ]
    for load in loads:
        load.start()

    barrier = pltpu.get_barrier_semaphore()

    @pl.loop(1, n)
    def _(k):
        pl.semaphore_signal(barrier, inc=1, device_id=ctx(after(k)), device_id_type=MESH_ID)

    for k in range(1, ny):
        pl.semaphore_signal(
            barrier, inc=1, device_id={TP: lax.rem(ty + k, ny)}, device_id_type=MESH_ID
        )
    for d in range(1, ndp):
        for k in range(nx):
            to = {DP: lax.rem(dp + d, ndp), CX: lax.rem(cx + k, nx)}
            pl.semaphore_signal(barrier, inc=1, device_id=to, device_id_type=MESH_ID)
    greeted = (n - 1) + (ny - 1) + (ndp - 1) * nx

    b = iota((8, 2 * length), 1)
    panel = (b >> lgp) & (n - 1)
    owner = jnp.zeros((8, 2 * length), I32)
    for i in range(n):
        owner = jnp.where(panel == i, plan_s[0, me * n + i] >> lgn, owner)
    target = owner * (2 * psz) + (b >> log2(length)) * psz + (b & (psz - 1))
    square = iota((2 * length, 2 * length), 0)
    fmat[...] = ones_where(square == target[0:1]).astype(BF)
    for load in loads[:3]:
        load.wait()
    x1[length : 2 * length] = (kv[...].astype(F32) * vv[...].astype(F32)).astype(BF)

    def to_blocks(value):
        return value.astype(BF).reshape(n, 2 * psz, cw)

    for c in range(CHUNKS):
        sbuf[c] = to_blocks(mm(fmat[...], x1[:, c * cw : (c + 1) * cw]))
        rbuf[c, me] = sbuf[c, me]

    pl.semaphore_wait(barrier, greeted)

    def send_blocks(src, dst, ssem, rsem):
        @pl.loop(1, n)
        def _(k):
            to = after(k)
            pltpu.make_async_remote_copy(
                src_ref=src.at[to],
                dst_ref=dst.at[me],
                send_sem=ssem,
                recv_sem=rsem,
                device_id=ctx(to),
                device_id_type=MESH_ID,
            ).start()

    def wait_bytes(ref, sem):
        pltpu.make_async_copy(ref, ref, sem).wait()

    loads[3].wait()
    ag = []
    for k in range(1, ny):
        copy = pltpu.make_async_remote_copy(
            src_ref=og.at[ty],
            dst_ref=og.at[ty],
            send_sem=ags.at[k],
            recv_sem=agr.at[k],
            device_id={TP: lax.rem(ty + k, ny)},
            device_id_type=MESH_ID,
        )
        copy.start()
        ag.append(copy)
    for c in range(CHUNKS):
        send_blocks(sbuf.at[c], rbuf.at[c], fs.at[c], fr.at[c])

    pv = plan_v[...]
    slot_of = jnp.where((pv >> lgn) == me, pv & (n - 1), 0).astype(F32)
    slot_of = jnp.broadcast_to(slot_of, (8, n * n)).astype(BF)
    gather = ones_where((iota((n * n, 2 * length), 0) >> lgn) == (iota((n * n, 2 * length), 1) >> (lgp + 1)))
    slot = mm(slot_of, gather.astype(BF)).astype(I32)
    target = ((b >> lgp) & 1) * length + slot * psz + (b & (psz - 1))
    pmat[...] = ones_where(square == target[0:1]).astype(BF)
    eye = ones_where(square == iota((2 * length, 2 * length), 1)).astype(BF)
    rmat[...] = mm_nt(eye, pmat[...]).astype(BF)
    hmat[...] = mm_nt(eye, fmat[...]).astype(BF)

    starts = []
    run = jnp.int32(0)
    for d in range(docs):
        starts.append(run)
        run = run + len_s[0, d]

    def documents(positions):
        count = jnp.zeros(positions.shape, I32)
        for start in starts:
            count = count + jnp.where(positions >= start, 1, 0)
        return jnp.where(positions >= total, docs + 1, count)

    base = me * length
    row = iota((taps, LANES), 0)
    lane = iota((taps, LANES), 1)
    lane8 = iota((8, (blocks + 2) * taps), 1)
    along = documents(base - taps + lane8)

    def same(doc_rows, first):
        return doc_rows == along[0:1, first : first + taps]

    for k in range(blocks):
        here = documents(base + k * taps + row)
        at = (k + 1) * taps
        mf[k, :, 0:taps] = ones_where(same(here, at - taps) & (lane > row))
        mf[k, :, taps : 2 * taps] = ones_where(same(here, at) & (lane <= row))
        mb[k, :, 0:taps] = ones_where(same(here, at) & (lane >= row))
        mb[k, :, taps : 2 * taps] = ones_where(same(here, at + taps) & (lane < row))
        back = taps - 1 - row
        here = documents(base + k * taps + back)
        mflip[k, :, 0:taps] = ones_where(same(here, at) & (lane >= back))
        mflip[k, :, taps : 2 * taps] = ones_where(same(here, at + taps) & (lane < back))

    filt = filt_v[...]
    turn = ones_where(((taps - row) & (taps - 1)) == lane).astype(BF)
    tap3[0] = filt.astype(F32)
    tap3[1] = mm(filt, turn)

    @pl.loop(0, cfg["groups"])
    def _(g):
        for t_ref, m_ref, which in ((tf, mf, 1), (tb, mb, 0)):
            taps_row = jnp.broadcast_to(tap3[which, pl.ds(g, 1), :], (taps, taps))
            circ = pltpu.roll(taps_row, 0, 1, stride=1, stride_axis=0)
            at = pl.ds(pl.multiple_of(g * taps, taps), taps)
            for k in range(blocks):
                t_ref[k, at, 0:taps] = (circ * m_ref[k, :, 0:taps]).astype(BF)
                t_ref[k, at, taps : 2 * taps] = (circ * m_ref[k, :, taps : 2 * taps]).astype(BF)

    loads[4].wait()

    def add_grad(source, first):
        @pl.loop(0, CHUNKS)
        def _(c):
            part = mm_nt(
                og[source],
                w[pl.ds(pl.multiple_of(c * cw, cw), cw), pl.ds(pl.multiple_of(source * width, width), width)],
            )
            gg[c] = part if first else gg[c] + part

    add_grad(ty, True)
    for k in range(1, ny):
        ag[k - 1].wait_recv()
        add_grad(lax.rem(ty - k + ny, ny), False)

    nxt, prv = ctx(after(1)), ctx(after(n - 1))
    halos = []

    def stage_a(c):
        wait_bytes(rbuf.at[c, pl.ds(0, n - 1)], fr.at[c])
        owned = mm(pmat[...], rbuf[c].reshape(2 * length, cw))
        query = owned[0:length]
        qo[c] = query.astype(BF)
        pw[c, taps : taps + length] = owned[length : 2 * length].astype(BF)
        cbw[c, 0:length] = (gg[c] * query).astype(BF)
        one = pltpu.make_async_remote_copy(
            src_ref=pw.at[c, pl.ds(length, taps)],
            dst_ref=pw.at[c, pl.ds(0, taps)],
            send_sem=phs.at[c],
            recv_sem=phr.at[c],
            device_id=nxt,
            device_id_type=MESH_ID,
        )
        two = pltpu.make_async_remote_copy(
            src_ref=cbw.at[c, pl.ds(0, taps)],
            dst_ref=cbw.at[c, pl.ds(length, taps)],
            send_sem=chs.at[c],
            recv_sem=chr_.at[c],
            device_id=prv,
            device_id_type=MESH_ID,
        )
        one.start()
        two.start()
        halos.append((one, two))

    group = lane >> log2(gsz)
    anti = ones_where(lane == taps - 1 - row).astype(BF)

    def pick(res):
        out = res[0:taps]
        for g in range(1, per):
            out = jnp.where(group == g, res[g * taps : (g + 1) * taps], out)
        return out

    def stage_b(c):
        for halo in halos[c]:
            halo.wait_recv()
        for j in range(cols):
            lanes = slice(j * LANES, (j + 1) * LANES)
            col = c * cols + j
            outer = [None] * per
            for k in range(blocks):
                own = slice(k * taps, (k + 1) * taps)
                win = slice(k * taps, (k + 2) * taps)
                t_rows = slice(col * rows, (col + 1) * rows)
                conv = pick(mm(tf[k, t_rows, :], pw[c, win, lanes]))
                gated[own, c * cw + j * LANES : c * cw + (j + 1) * LANES] = (
                    qo[c, own, lanes].astype(F32) * conv
                ).astype(BF)
                x2[c, own, lanes] = (gg[c, own, lanes] * conv).astype(BF)
                x2[c, length + k * taps : length + (k + 1) * taps, lanes] = pick(
                    mm(tb[k, t_rows, :], cbw[c, win, lanes])
                ).astype(BF)
                flipped = mm(anti, pw[c, (k + 1) * taps : (k + 2) * taps, lanes])
                stacked = jnp.concatenate(
                    [jnp.where(group == g, flipped, 0.0).astype(BF) for g in range(per)], axis=0
                )
                res = mm_nt(stacked, cbw[c, win, lanes])
                for g in range(per):
                    part = res[g * taps : (g + 1) * taps]
                    term = part[:, 0:taps] * mflip[k, :, 0:taps] + part[:, taps:] * mflip[k, :, taps:]
                    outer[g] = term if k == 0 else outer[g] + term
            tap[col] = jnp.concatenate(
                [
                    jnp.sum(pltpu.roll(o, 1, 1, stride=1, stride_axis=0), axis=0, keepdims=True)
                    for o in outer
                ],
                axis=0,
            )
        sbuf2[c] = to_blocks(mm(rmat[...], x2[c]))
        rbuf2[c, me] = sbuf2[c, me]
        send_blocks(sbuf2.at[c], rbuf2.at[c], bs.at[c], br.at[c])

        @pl.loop(0, ny)
        def _(y):
            at = pl.ds(pl.multiple_of(y * width, width), width)
            part = mm(gated[:, c * cw : (c + 1) * cw], w[c * cw : (c + 1) * cw, at])
            acc[y] = part if c == 0 else acc[y] + part

    for c in range(CHUNKS):
        stage_a(c)
    for c in range(CHUNKS):
        stage_b(c)

    rs = []
    for k in range(1, ny):
        to = lax.rem(ty + k, ny)
        rs_send[k] = acc[to].astype(BF)
        copy = pltpu.make_async_remote_copy(
            src_ref=rs_send.at[k],
            dst_ref=rs_recv.at[ty],
            send_sem=rss.at[k],
            recv_sem=rsr.at[k],
            device_id={TP: to},
            device_id_type=MESH_ID,
        )
        copy.start()
        rs.append(copy)
    rs_recv[ty] = acc[ty].astype(BF)

    firsts = []
    for k in range(1, group_n):
        to = lax.rem(e_me + k, group_n)
        copy = pltpu.make_async_remote_copy(
            src_ref=tap.at[to],
            dst_ref=tap1.at[e_me],
            send_sem=t1s.at[k],
            recv_sem=t1r.at[k],
            device_id=peer_e(to),
            device_id_type=MESH_ID,
        )
        copy.start()
        firsts.append(copy)
    tap1[e_me] = tap[e_me]
    for copy in firsts:
        copy.wait_recv()
    tap2[cz] = jnp.sum(tap1[...], axis=0)
    seconds = []
    for k in range(1, nz):
        copy = pltpu.make_async_remote_copy(
            src_ref=tap2.at[cz],
            dst_ref=tap2.at[cz],
            send_sem=t2s.at[k],
            recv_sem=t2r.at[k],
            device_id={CZ: lax.rem(cz + k, nz)},
            device_id_type=MESH_ID,
        )
        copy.start()
        seconds.append(copy)
    for copy in seconds:
        copy.wait_recv()
    summed = tap2[0]
    for z in range(1, nz):
        summed = summed + tap2[z]
    scale = 1.0 / math.sqrt(float(ndp * total))
    fg_o[e_me] = summed * scale
    thirds = []
    for k in range(1, group_n):
        copy = pltpu.make_async_remote_copy(
            src_ref=fg_o.at[e_me],
            dst_ref=fg_o.at[e_me],
            send_sem=t3s.at[k],
            recv_sem=t3r.at[k],
            device_id=peer_e(lax.rem(e_me + k, group_n)),
            device_id_type=MESH_ID,
        )
        copy.start()
        thirds.append(copy)

    for c in range(CHUNKS):
        wait_bytes(rbuf2.at[c, pl.ds(0, n - 1)], br.at[c])
        home = mm(hmat[...], rbuf2[c].reshape(2 * length, cw))
        at = slice(c * cw, (c + 1) * cw)
        qg_o[:, at] = home[0:length].astype(BF)
        kg_o[:, at] = (home[length:] * vv[:, at].astype(F32)).astype(BF)
        vg_o[:, at] = (home[length:] * kv[:, at].astype(F32)).astype(BF)
    for copy in rs:
        copy.wait_recv()
    summed = rs_recv[0].astype(F32)
    for y in range(1, ny):
        summed = summed + rs_recv[y].astype(F32)
    mixed_o[...] = summed.astype(BF)
    for copy in thirds:
        copy.wait_recv()

    for copy in ag + rs + firsts + seconds + thirds:
        copy.wait_send()
    for one, two in halos:
        one.wait_send()
        two.wait_send()
    for c in range(CHUNKS):
        wait_bytes(sbuf.at[c, pl.ds(0, n - 1)], fs.at[c])
        wait_bytes(sbuf2.at[c, pl.ds(0, n - 1)], bs.at[c])


def build(mesh, nx, nz):
    ndp, ny = mesh.shape["dp"], mesh.shape["tensor"]
    n = nx * nz
    finer = Mesh(mesh.devices.reshape(ndp, nx, nz, ny), (DP, CX, CZ, TP))

    def per_device(query, key, value, filters, weight, lengths, plan, out_grad):
        length, width = query.shape[1:]
        groups, taps = filters.shape
        cfg = dict(
            n=n, nx=nx, nz=nz, ny=ny, ndp=ndp, length=length, width=width, taps=taps,
            docs=lengths.shape[1], groups=groups,
        )
        cw, blocks, psz = width // CHUNKS, length // taps, length // n
        vmem = pl.BlockSpec(memory_space=pltpu.VMEM)
        smem = pl.BlockSpec(memory_space=pltpu.SMEM)
        hbm = pl.BlockSpec(memory_space=pl.ANY)
        dma = pltpu.SemaphoreType.DMA
        row = jax.ShapeDtypeStruct((length, width), BF)
        e = ndp * nx
        assert groups == e * 8
        outs = pl.pallas_call(
            functools.partial(layer_kernel, cfg),
            name="layer",
            out_shape=(row, row, row, row, jax.ShapeDtypeStruct((e, 8, taps), F32)),
            in_specs=[smem, smem, vmem, vmem, hbm, hbm, hbm, hbm, hbm],
            out_specs=(vmem,) * 5,
            scratch_shapes=[
                pltpu.VMEM((2 * length, width), BF),
                pltpu.VMEM((length, width), BF),
                pltpu.VMEM((length, width), BF),
                pltpu.VMEM(weight.shape, BF),
                pltpu.VMEM((ny, length, width), BF),
                *[pltpu.VMEM((2 * length, 2 * length), BF)] * 4,
                *[pltpu.VMEM((CHUNKS, n, 2 * psz, cw), BF)] * 4,
                pltpu.VMEM((CHUNKS, length, cw), BF),
                *[pltpu.VMEM((CHUNKS, length + taps, cw), BF)] * 2,
                pltpu.VMEM((CHUNKS, 2 * length, cw), BF),
                pltpu.VMEM((length, width), BF),
                pltpu.VMEM((CHUNKS, length, cw), F32),
                pltpu.VMEM((ny, length, width), F32),
                *[pltpu.VMEM((blocks, groups * taps, 2 * taps), BF)] * 2,
                *[pltpu.VMEM((blocks, taps, 2 * taps), F32)] * 3,
                *[pltpu.VMEM((ny, length, width), BF)] * 2,
                *[pltpu.VMEM((e, 8, taps), F32)] * 2,
                pltpu.VMEM((nz, 8, taps), F32),
                pltpu.VMEM((2, groups, taps), F32),
                dma((5,)),
                dma((CHUNKS,)), dma((CHUNKS,)),
                dma((ny,)), dma((ny,)),
                *[dma((CHUNKS,))] * 4,
                dma((CHUNKS,)), dma((CHUNKS,)),
                dma((ny,)), dma((ny,)),
                dma((e,)), dma((e,)),
                dma((nz,)), dma((nz,)),
                dma((e,)), dma((e,)),
            ],
            compiler_params=pltpu.CompilerParams(
                collective_id=0, has_side_effects=True, vmem_limit_bytes=67043328
            ),
        )(plan, lengths, plan, filters, query[0], key[0], value[0], out_grad[0], weight)
        mixed, qg, kg, vg, fg = outs
        return mixed[None], qg[None], kg[None], vg[None], fg.reshape(groups, taps)

    rows = P(DP, CONTEXT, TP)
    split = P(TP, None)
    return jax.shard_map(
        per_device,
        mesh=finer,
        in_specs=(rows, rows, rows, split, split, P(DP, None), P(DP, None), rows),
        out_specs=(rows, rows, rows, rows, split),
        check_vma=False,
    )


def solution(mesh):
    return build(mesh, 4, mesh.shape["context"] // 4)
```

time: 224 us -> 95.2 us (0.42)
  Pallas kernels: 0 us -> 84.5 us
  matrix products: 57.4 us -> 0 us
  blocking collectives: 50.9 us -> 0 us
  starting transfers between devices: 37.8 us -> 0 us
  local copies, waits for them, and re-layouts: 37.6 us -> 8.84 us
  other arithmetic: 26.2 us -> 0 us
  waiting for transfers between devices: 9.28 us -> 0 us
    pallas_call x0 -> x1, Pallas kernels: none -> 84.5 us  [per_device(): pl.pallas_call(functools.partial(layer_kernel, cfg), name='layer', out_sh...]
    dot_general x20 -> x0, matrix products: 57.4 us -> none  [the longest x2 9.74 us: band_matrix(): jnp.dot(filters, tap_table.reshape(taps, -1), preferred_element_type=jnp....]
    psum x3 -> x0, blocking collectives: 50.9 us -> none  [over_axes(): shard = lax.psum(shard, axis)]
    all_to_all x4 -> x0, starting transfers between devices: 32.4 us -> none  [the longest x2 22.6 us: sent_together(): lax.all_to_all(both, axis, split_axis=split_dim, concat_axis=concat_dim,...]
    mul x2 -> x0, other arithmetic: 10.7 us -> none  [the longest x1 6.02 us: per_device(): back_masked = bwd_band[None] * bwd_mask[:, None].astype(jnp.bfloat16)]
    reshape x10 -> x0, local copies, waits for them, and re-layouts: 8.8 us -> none  [the longest x6 5.37 us: regroup(): flat = rows_in.reshape(count, -1)]
    all_to_all x4 -> x0, waiting for transfers between devices: 6.2 us -> none  [the longest x1 3.94 us: from_everyone(): return lax.all_to_all(copies, axis, split_axis=0, concat_axis=0, tiled=True)]
    unnamed x55 -> x5, local copies, waits for them, and re-layouts: 14.4 us -> 8.84 us
  transfers between devices with their start and end apart: 6 -> 0, of which waited for: 3 -> 0; matrix products, arithmetic and copies ran while one was open for 44% -> 0% of each run, Pallas kernels for 0% -> 0%
where the time goes in v1:
time: 95.2 us; the launch traced here: 94 us
  Pallas kernels  84.5 us (89%)
  local copies, waits for them, and re-layouts  8.84 us (9%)
    pallas_call x1, Pallas kernels, per_device(): pl.pallas_call(functools.partial(layer_kernel, cfg), name='layer', out_sh...  84.5 us
    unnamed x5, local copies, waits for them, and re-layouts  8.84 us

profile of v1, /device:TPU:8, one launch (start us, length us, event | category | flops | bytes accessed | tf_op | source)
XLA Modules:
  0.0 94.0 jit_solution(8586142759464862930)
XLA Ops:
  0.6 84.5 %layer.1 = (bf16[256,1024]{1,0:T(8,128)(2,1)}, bf16[256,1024]{1,0:T(8,128)(2,1)}, bf16[256,1024]{1,0:T(8,128)(2,1)}, bf16[256,1024]{1,0:T(8,128)(2,1)}, f32[8,8,128]{2,1,0:T(8,128)}) custom-call(s32[1,1024]{1,0:T(1,128)} %plan_v.1, s32[1,32]{1,0:T(1,128)} %len_s.1, s32[1,1024]{1,0:T(1,128)} %plan_v.1, bf16[64,128]{1,0:T(8,128)(2,1)} %filt_v.1, ...), custom_call_target="tpu_custom_call" | custom-call | tf_op jit(solution)/shard_map/layer/pallas_call | solution.py:435
  85.1 1.9 %copy.18 = bf16[1,256,1024]{2,1,0:T(8,128)(2,1)} copy(bf16[1,256,1024]{2,1,0:T(8,128)(2,1)} %bitcast.16) | data formatting | bytes 1048576
  87.0 1.9 %copy.19 = bf16[1,256,1024]{2,1,0:T(8,128)(2,1)} copy(bf16[1,256,1024]{2,1,0:T(8,128)(2,1)} %bitcast.15) | data formatting | bytes 1048576
  88.9 1.9 %copy.20 = bf16[1,256,1024]{2,1,0:T(8,128)(2,1)} copy(bf16[1,256,1024]{2,1,0:T(8,128)(2,1)} %bitcast.14) | data formatting | bytes 1048576
  90.7 1.9 %copy.21 = bf16[1,256,1024]{2,1,0:T(8,128)(2,1)} copy(bf16[1,256,1024]{2,1,0:T(8,128)(2,1)} %bitcast.13) | data formatting | bytes 1048576
  92.6 1.4 %copy.22 = f32[64,128]{1,0:T(8,128)} copy(f32[64,128]{1,0:T(8,128)} %bitcast.17) | data formatting | bytes 65536

commit v2 on v1

v2 whole, which is shorter than its diff:
```python
import contextlib
import functools
import math

import jax
import jax.numpy as jnp
from jax import lax
from jax.experimental import pallas as pl
from jax.experimental.pallas import tpu as pltpu
from jax.sharding import Mesh
from jax.sharding import PartitionSpec as P

DP, CX, CZ, TP = "dp", "context_0", "context_1", "tensor"
CONTEXT = (CX, CZ)
BF = jnp.bfloat16
F32 = jnp.float32
I32 = jnp.int32
LANES = 128
HALVES = 2
UNITS = 4
MESH_ID = pl.DeviceIdType.MESH
NT = (((1,), (1,)), ((), ()))


def mark(name):
    return contextlib.nullcontext()


def log2(n):
    return n.bit_length() - 1


def iota(shape, dim):
    return lax.broadcasted_iota(I32, shape, dim)


def ones_where(cond):
    return jnp.where(cond, 1.0, 0.0)


def mm(a, b):
    return jnp.dot(a, b, preferred_element_type=F32)


def mm_nt(a, b):
    return lax.dot_general(a, b, NT, preferred_element_type=F32)


def layer_kernel(
    cfg,
    plan_hbm, len_hbm, filt_hbm, q_hbm, k_hbm, v_hbm, og_hbm, w_hbm,
    mixed_h, qg_h, kg_h, vg_h, fg_h,
    plan_s, len_s, plan_v, filt_v, mixed_o, qg_o, kg_o, vg_o, fg_o,
    xp, xq, kv, vv, w, og, fmat, hmat, pmat, rmat, sbuf, rbuf, sbuf2, rbuf2,
    qo, pw, cbw, x2, gated, conv, gg, acc, tf, tb, mf, mb, mflip,
    rs_send, rs_recv, tap, tap1, tap2, tap3,
    small, out_sem, ld, fs, fr, ags, agr, phs, phr, chs, chr_, bs, br, rss, rsr, t1s, t1r, t2s, t2r, t3s, t3r,
):
    n, nx, nz, ny, ndp = cfg["n"], cfg["nx"], cfg["nz"], cfg["ny"], cfg["ndp"]
    length, width, taps, docs = cfg["length"], cfg["width"], cfg["taps"], cfg["docs"]
    psz, gsz, total = length // n, 16, length * n
    hw = width // HALVES
    uw = hw // 2
    cols = hw // LANES
    blocks = length // taps
    per = LANES // gsz
    rows = per * taps
    lgn, lgp = log2(n), log2(psz)

    dp, cx, cz, ty = (lax.axis_index(a) for a in (DP, CX, CZ, TP))
    me = cx * nz + cz
    group_n = ndp * nx
    e_me = dp * nx + cx

    def ctx(index):
        return {CX: index // nz, CZ: lax.rem(index, nz)}

    def peer_e(index):
        return {DP: index // nx, CX: lax.rem(index, nx)}

    def after(k):
        return lax.rem(me + k, n)

    barrier = pltpu.get_barrier_semaphore()

    @pl.loop(1, n)
    def _(k):
        pl.semaphore_signal(barrier, inc=1, device_id=ctx(after(k)), device_id_type=MESH_ID)

    for k in range(1, ny):
        pl.semaphore_signal(
            barrier, inc=1, device_id={TP: lax.rem(ty + k, ny)}, device_id_type=MESH_ID
        )
    for d in range(1, ndp):
        for k in range(nx):
            to = {DP: lax.rem(dp + d, ndp), CX: lax.rem(cx + k, nx)}
            pl.semaphore_signal(barrier, inc=1, device_id=to, device_id_type=MESH_ID)
    greeted = (n - 1) + (ny - 1) + (ndp - 1) * nx

    moves = [(k_hbm, kv), (v_hbm, vv), (og_hbm, og.at[ty])]
    for h in range(HALVES):
        for p in range(2):
            moves.append((q_hbm.at[:, pl.ds(h * hw + p * uw, uw)], xq.at[h, pl.ds(p * length, length)]))
    moves.append((w_hbm, w))
    loads = [pltpu.make_async_copy(src, dst, ld.at[i]) for i, (src, dst) in enumerate(moves)]
    smalls = [
        pltpu.make_async_copy(src, dst, small.at[i])
        for i, (src, dst) in enumerate(
            [(plan_hbm, plan_s), (plan_hbm, plan_v), (filt_hbm, filt_v), (len_hbm, len_s)]
        )
    ]
    for load in smalls[:1] + loads[:2] + smalls[1:] + loads[2:]:
        load.start()

    smalls[0].wait()

    b = iota((8, 2 * length), 1)
    panel = (b >> lgp) & (n - 1)
    owner = jnp.zeros((8, 2 * length), I32)
    for i in range(n):
        owner = jnp.where(panel == i, plan_s[0, me * n + i] >> lgn, owner)
    target = owner * (2 * psz) + (b >> log2(length)) * psz + (b & (psz - 1))
    square = iota((2 * length, 2 * length), 0)
    fmat[...] = ones_where(square == target[0:1]).astype(BF)
    for load in loads[:2]:
        load.wait()

    def to_blocks(value):
        return value.astype(BF).reshape(n, 2 * psz, uw)

    for h in range(HALVES):
        for p in range(2):
            at = slice(h * hw + p * uw, h * hw + (p + 1) * uw)
            xp[h, p * length : (p + 1) * length] = (
                kv[:, at].astype(F32) * vv[:, at].astype(F32)
            ).astype(BF)
        sbuf[h] = to_blocks(mm(fmat[...], xp[h]))
        rbuf[h, me] = sbuf[h, me]

    with mark("barrier"):
        pl.semaphore_wait(barrier, greeted)

    def start(src, dst, ssem, rsem, to):
        copy = pltpu.make_async_remote_copy(
            src_ref=src,
            dst_ref=dst,
            send_sem=ssem,
            recv_sem=rsem,
            device_id=to,
            device_id_type=MESH_ID,
        )
        copy.start()
        return copy

    def send_blocks(src, dst, ssem, rsem):
        @pl.loop(1, n)
        def _(k):
            to = after(k)
            start(src.at[to], dst.at[me], ssem, rsem, ctx(to))

    def send_forward(u):
        with mark("send"):
            send_blocks(sbuf.at[u], rbuf.at[u], fs.at[u], fr.at[u])

    def wait_bytes(ref, sem):
        pltpu.make_async_copy(ref, ref, sem).wait()

    half = length // 2
    up, down = {TP: lax.rem(ty + 1, ny)}, {TP: lax.rem(ty + ny - 1, ny)}
    below, above = lax.rem(ty + ny - 1, ny), lax.rem(ty + 1, ny)
    across = lax.rem(ty + 2, ny)
    first, second = pl.ds(0, half), pl.ds(half, half)

    def pass_on(source, part, to, i):
        piece = og.at[source, part]
        return start(piece, piece, ags.at[i], agr.at[i], to)

    loads[2].wait()
    ag = [
        pass_on(ty, first, up, 0),
        pass_on(ty, second, down, 1),
        pass_on(ty, second, up, 2),
        pass_on(ty, first, down, 3),
    ]
    send_forward(0)
    send_forward(1)
    for h in range(HALVES):
        for load in loads[3 + 2 * h : 5 + 2 * h]:
            load.wait()
        sbuf[HALVES + h] = to_blocks(mm(fmat[...], xq[h]))
        rbuf[HALVES + h, me] = sbuf[HALVES + h, me]

    for load in smalls[1:]:
        load.wait()
    pv = plan_v[...]
    slot_of = jnp.where((pv >> lgn) == me, pv & (n - 1), 0).astype(F32)
    slot_of = jnp.broadcast_to(slot_of, (8, n * n)).astype(BF)
    table = (n * n, 2 * length)
    gather = ones_where((iota(table, 0) >> lgn) == (iota(table, 1) >> (lgp + 1)))
    slot = mm(slot_of, gather.astype(BF)).astype(I32)
    target = ((b >> lgp) & 1) * length + slot * psz + (b & (psz - 1))
    pmat[...] = ones_where(square == target[0:1]).astype(BF)

    starts = []
    run = jnp.int32(0)
    for d in range(docs):
        starts.append(run)
        run = run + len_s[0, d]

    def documents(positions):
        count = jnp.zeros(positions.shape, I32)
        for begin in starts:
            count = count + jnp.where(positions >= begin, 1, 0)
        return jnp.where(positions >= total, docs + 1, count)

    base = me * length
    row = iota((taps, LANES), 0)
    lane = iota((taps, LANES), 1)
    lane8 = iota((8, (blocks + 2) * taps), 1)
    along = documents(base - taps + lane8)

    def same(doc_rows, at):
        return doc_rows == along[0:1, at : at + taps]

    for k in range(blocks):
        here = documents(base + k * taps + row)
        at = (k + 1) * taps
        mf[k, :, 0:taps] = ones_where(same(here, at - taps) & (lane > row))
        mf[k, :, taps : 2 * taps] = ones_where(same(here, at) & (lane <= row))
        mb[k, :, 0:taps] = ones_where(same(here, at) & (lane >= row))
        mb[k, :, taps : 2 * taps] = ones_where(same(here, at + taps) & (lane < row))
        back = taps - 1 - row
        here = documents(base + k * taps + back)
        mflip[k, :, 0:taps] = ones_where(same(here, at - taps) & (lane > back))
        mflip[k, :, taps : 2 * taps] = ones_where(same(here, at) & (lane <= back))

    filt = filt_v[...]
    turn = ones_where(((taps - row) & (taps - 1)) == lane).astype(BF)
    tap3[0] = filt.astype(F32)
    tap3[1] = mm(filt, turn)

    def circulants(t_ref, m_ref, which):
        with mark("toep"):

            @pl.loop(0, cfg["groups"], step=4)
            def _(first_group):
                for i in range(4):
                    g = first_group + i
                    taps_row = jnp.broadcast_to(tap3[which, pl.ds(g, 1), :], (taps, taps))
                    circ = pltpu.roll(taps_row, 0, 1, stride=1, stride_axis=0)
                    at = pl.ds(pl.multiple_of(g * taps, taps), taps)
                    for k in range(blocks):
                        for h in range(2):
                            part = slice(h * taps, (h + 1) * taps)
                            t_ref[k, at, part] = (circ * m_ref[k, :, part]).astype(BF)

    def add_grad(source, opening):
        with mark("gg"):

            @pl.loop(0, 2 * HALVES)
            def _(c):
                part = mm_nt(
                    og[source],
                    w[
                        pl.ds(pl.multiple_of(c * uw, uw), uw),
                        pl.ds(pl.multiple_of(source * width, width), width),
                    ],
                )
                gg[c] = part if opening else gg[c] + part

    nxt, prv = ctx(after(1)), ctx(after(n - 1))
    prod_halo, back_halo = [], []

    def arrived(u):
        with mark(f"fwait{u}"):
            wait_bytes(rbuf.at[u, pl.ds(0, n - 1)], fr.at[u])
        owned = mm(pmat[...], rbuf[u].reshape(2 * length, uw)).astype(BF)
        return owned[0:length], owned[length : 2 * length]

    def receive_product(h):
        pw[h, taps : taps + length, 0:uw], pw[h, taps : taps + length, uw:hw] = arrived(h)
        prod_halo.append(
            start(pw.at[h, pl.ds(length, taps)], pw.at[h, pl.ds(0, taps)], phs.at[h], phr.at[h], nxt)
        )
        send_forward(HALVES + h)

    def receive_query(h):
        for p, part in enumerate(arrived(HALVES + h)):
            qo[2 * h + p] = part
            cbw[h, 0:length, p * uw : (p + 1) * uw] = (
                gg[2 * h + p] * part.astype(F32)
            ).astype(BF)
        back_halo.append(
            start(cbw.at[h, pl.ds(0, taps)], cbw.at[h, pl.ds(length, taps)], chs.at[h], chr_.at[h], prv)
        )

    group = lane >> log2(gsz)
    anti = ones_where(lane == taps - 1 - row).astype(BF)

    def pick(res):
        out = res[0:taps]
        for g in range(1, per):
            out = jnp.where(group == g, res[g * taps : (g + 1) * taps], out)
        return out

    def each_tile(h):
        for j in range(cols):
            lanes = slice(j * LANES, (j + 1) * LANES)
            col = h * cols + j
            for k in range(blocks):
                own = slice(k * taps, (k + 1) * taps)
                win = slice(k * taps, (k + 2) * taps)
                yield j, col, k, lanes, own, win, slice(col * rows, (col + 1) * rows)

    def placed(j, k):
        p, at = (j * LANES) // uw, (j * LANES) % uw
        return p, slice(p * length + k * taps, p * length + (k + 1) * taps), slice(at, at + LANES)

    def filter_forward(h):
        with mark(f"phalo{h}"):
            prod_halo[h].wait_recv()
        with mark("conv"):
            for j, col, k, lanes, own, win, t_rows in each_tile(h):
                p, _, at = placed(j, k)
                conv[2 * h + p, own, at] = pick(mm(tf[k, t_rows, :], pw[h, win, lanes]))

    def pack_back(u):
        sbuf2[u] = to_blocks(mm(rmat[...], x2[u]))
        rbuf2[u, me] = sbuf2[u, me]

    def query_back(h):
        with mark("qback"):
            for p in range(2):
                x2[h, p * length : (p + 1) * length] = (gg[2 * h + p] * conv[2 * h + p]).astype(BF)
            pack_back(h)

    def gate(h):
        for p in range(2):
            at = slice(h * hw + p * uw, h * hw + (p + 1) * uw)
            gated[:, at] = (qo[2 * h + p].astype(F32) * conv[2 * h + p]).astype(BF)

    def project(y, h):
        at = pl.ds(pl.multiple_of(y * width, width), width)
        rows_in = slice(h * hw, (h + 1) * hw)
        return mm(gated[:, rows_in], w[rows_in, at])

    def product_back(h):
        u = HALVES + h
        with mark(f"chalo{h}"):
            back_halo[h].wait_recv()
        with mark("pback"):
            for j, _, k, lanes, _, win, t_rows in each_tile(h):
                _, to, at = placed(j, k)
                x2[u, to, at] = pick(mm(tb[k, t_rows, :], cbw[h, win, lanes])).astype(BF)
            pack_back(u)

    def send_back(u):
        with mark("send2"):
            send_blocks(sbuf2.at[u], rbuf2.at[u], bs.at[u], br.at[u])

    def filter_terms(h):
        with mark("terms"):
            for _, col, k, lanes, own, win, _ in each_tile(h):
                if k == 0:
                    outer = [None] * per
                flipped = mm(anti, cbw[h, own, lanes])
                stacked = jnp.concatenate(
                    [jnp.where(group == g, flipped, 0.0).astype(BF) for g in range(per)], axis=0
                )
                res = mm_nt(stacked, pw[h, win, lanes])
                for g in range(per):
                    part = res[g * taps : (g + 1) * taps]
                    term = (
                        part[:, 0:taps] * mflip[k, :, 0:taps]
                        + part[:, taps:] * mflip[k, :, taps:]
                    )
                    outer[g] = term if k == 0 else outer[g] + term
                if k == blocks - 1:
                    turned = [pltpu.roll(o, 0, 1, stride=1, stride_axis=0) for o in outer]
                    tap[col] = jnp.concatenate(
                        [jnp.sum(o, axis=0, keepdims=True) for o in turned], axis=0
                    )

    circulants(tf, mf, 1)
    receive_product(0)
    with mark("agw"):
        ag[0].wait_recv()
        ag.append(pass_on(below, first, up, 4))
        ag[1].wait_recv()
        ag.append(pass_on(above, second, down, 5))
    eye = ones_where(square == iota((2 * length, 2 * length), 1)).astype(BF)
    rmat[...] = mm_nt(eye, pmat[...]).astype(BF)
    hmat[...] = mm_nt(eye, fmat[...]).astype(BF)
    with mark("wwait"):
        loads[-1].wait()
    add_grad(ty, True)
    receive_product(1)
    circulants(tb, mb, 0)
    filter_forward(0)
    with mark("agw2"):
        ag[2].wait_recv()
        ag[3].wait_recv()
    add_grad(below, False)
    add_grad(above, False)
    with mark("agw3"):
        ag[4].wait_recv()
        ag[5].wait_recv()
    add_grad(across, False)
    query_back(0)
    send_back(0)
    receive_query(0)
    gate(0)
    with mark("proj"):

        @pl.loop(0, ny)
        def _(y):
            acc[y] = project(y, 0)

    filter_terms(0)
    filter_forward(1)
    query_back(1)
    receive_query(1)
    gate(1)

    rs = []
    with mark("proj"):
        for k in range(1, ny):
            to = lax.rem(ty + k, ny)
            rs_send[k] = (acc[to] + project(to, 1)).astype(BF)
            rs.append(start(rs_send.at[k], rs_recv.at[ty], rss.at[k], rsr.at[k], {TP: to}))
        rs_recv[ty] = (acc[ty] + project(ty, 1)).astype(BF)

    filter_terms(1)
    firsts = []
    for k in range(1, group_n):
        to = lax.rem(e_me + k, group_n)
        firsts.append(start(tap.at[to], tap1.at[e_me], t1s.at[k], t1r.at[k], peer_e(to)))
    tap1[e_me] = tap[e_me]
    send_back(1)

    product_back(0)
    send_back(2)
    product_back(1)
    with mark("t1wait"):
        for copy in firsts:
            copy.wait_recv()
    tap2[cz] = jnp.sum(tap1[...], axis=0)
    seconds = []
    for k in range(1, nz):
        to = {CZ: lax.rem(cz + k, nz)}
        seconds.append(start(tap2.at[cz], tap2.at[cz], t2s.at[k], t2r.at[k], to))
    send_back(3)

    leaving = []

    def leave(src, dst):
        copy = pltpu.make_async_copy(src, dst, out_sem.at[len(leaving)])
        copy.start()
        leaving.append(copy)

    def loader_rows(u):
        h = u % HALVES
        with mark(f"bwait{u}"):
            wait_bytes(rbuf2.at[u, pl.ds(0, n - 1)], br.at[u])
        home = mm(hmat[...], rbuf2[u].reshape(2 * length, uw))
        for p in range(2):
            part = home[p * length : (p + 1) * length]
            at = slice(h * hw + p * uw, h * hw + (p + 1) * uw)
            if u < HALVES:
                qg_o[:, at] = part.astype(BF)
            else:
                kg_o[:, at] = (part * vv[:, at].astype(F32)).astype(BF)
                vg_o[:, at] = (part * kv[:, at].astype(F32)).astype(BF)
        at = pl.ds(h * hw, hw)
        for held, out in [(qg_o, qg_h)] if u < HALVES else [(kg_o, kg_h), (vg_o, vg_h)]:
            leave(held.at[:, at], out.at[:, at])

    loader_rows(0)
    loader_rows(1)
    with mark("t2wait"):
        for copy in seconds:
            copy.wait_recv()
    summed = tap2[0]
    for z in range(1, nz):
        summed = summed + tap2[z]
    scale = 1.0 / math.sqrt(float(ndp * total))
    mirror = ones_where(lane == taps - 1 - row)
    fg_o[e_me] = scale * jnp.dot(
        summed, mirror, precision=lax.Precision.HIGHEST, preferred_element_type=F32
    )
    thirds = []
    for k in range(1, group_n):
        to = peer_e(lax.rem(e_me + k, group_n))
        thirds.append(start(fg_o.at[e_me], fg_o.at[e_me], t3s.at[k], t3r.at[k], to))
    loader_rows(2)
    with mark("rswait"):
        for copy in rs:
            copy.wait_recv()
    summed = rs_recv[0].astype(F32)
    for y in range(1, ny):
        summed = summed + rs_recv[y].astype(F32)
    mixed_o[...] = summed.astype(BF)
    leave(mixed_o, mixed_h)
    with mark("t3wait"):
        for copy in thirds:
            copy.wait_recv()
    leave(fg_o, fg_h)
    loader_rows(3)

    with mark("drain"):
        for copy in ag + rs + prod_halo + back_halo + firsts + seconds + thirds:
            copy.wait_send()
        for u in range(UNITS):
            wait_bytes(sbuf.at[u, pl.ds(0, n - 1)], fs.at[u])
            wait_bytes(sbuf2.at[u, pl.ds(0, n - 1)], bs.at[u])
        for copy in leaving:
            copy.wait()


def hand_over(*refs):
    count = (len(refs) - 2) // 3
    srcs, dsts, held = refs[:count], refs[count : 2 * count], refs[2 * count : 3 * count]
    sem_in, sem_out = refs[3 * count :]
    ins = [pltpu.make_async_copy(a, b, sem_in.at[i]) for i, (a, b) in enumerate(zip(srcs, held, strict=True))]
    outs = [pltpu.make_async_copy(b, a, sem_out.at[i]) for i, (a, b) in enumerate(zip(dsts, held, strict=True))]
    for copy in ins:
        copy.start()
    for arrive, leave in zip(ins, outs, strict=True):
        arrive.wait()
        leave.start()
    for copy in outs:
        copy.wait()


def build(mesh, nx, nz):
    ndp, ny = mesh.shape["dp"], mesh.shape["tensor"]
    n = nx * nz
    finer = Mesh(mesh.devices.reshape(ndp, nx, nz, ny), (DP, CX, CZ, TP))

    def per_device(query, key, value, filters, weight, lengths, plan, out_grad):
        length, width = query.shape[1:]
        groups, taps = filters.shape
        cfg = dict(
            n=n, nx=nx, nz=nz, ny=ny, ndp=ndp, length=length, width=width, taps=taps,
            docs=lengths.shape[1], groups=groups,
        )
        hw, blocks, psz = width // HALVES, length // taps, length // n
        uw = hw // 2
        hbm = pl.BlockSpec(memory_space=pl.ANY)
        dma = pltpu.SemaphoreType.DMA
        row = jax.ShapeDtypeStruct((length, width), BF)
        e = ndp * nx
        assert groups == e * 8
        outs = pl.pallas_call(
            functools.partial(layer_kernel, cfg),
            name="layer",
            out_shape=[row, row, row, row, jax.ShapeDtypeStruct((e, 8, taps), F32)],
            in_specs=[hbm] * 8,
            out_specs=[hbm] * 5,
            scratch_shapes=[
                pltpu.SMEM(plan.shape, I32),
                pltpu.SMEM(lengths.shape, I32),
                pltpu.VMEM(plan.shape, I32),
                pltpu.VMEM(filters.shape, BF),
                *[pltpu.VMEM((length, width), BF)] * 4,
                pltpu.VMEM((e, 8, taps), F32),
                *[pltpu.VMEM((HALVES, 2 * length, uw), BF)] * 2,
                pltpu.VMEM((length, width), BF),
                pltpu.VMEM((length, width), BF),
                pltpu.VMEM(weight.shape, BF),
                pltpu.VMEM((ny, length, width), BF),
                *[pltpu.VMEM((2 * length, 2 * length), BF)] * 4,
                *[pltpu.VMEM((UNITS, n, 2 * psz, uw), BF)] * 4,
                pltpu.VMEM((2 * HALVES, length, uw), BF),
                *[pltpu.VMEM((HALVES, length + taps, hw), BF)] * 2,
                pltpu.VMEM((UNITS, 2 * length, uw), BF),
                pltpu.VMEM((length, width), BF),
                *[pltpu.VMEM((2 * HALVES, length, uw), F32)] * 2,
                pltpu.VMEM((ny, length, width), F32),
                *[pltpu.VMEM((blocks, groups * taps, 2 * taps), BF)] * 2,
                *[pltpu.VMEM((blocks, taps, 2 * taps), F32)] * 3,
                *[pltpu.VMEM((ny, length, width), BF)] * 2,
                *[pltpu.VMEM((e, 8, taps), F32)] * 2,
                pltpu.VMEM((nz, 8, taps), F32),
                pltpu.VMEM((2, groups, taps), F32),
                dma((4,)), dma((8,)), dma((8,)),
                dma((UNITS,)), dma((UNITS,)),
                dma((6,)), dma((6,)),
                *[dma((HALVES,))] * 4,
                dma((UNITS,)), dma((UNITS,)),
                dma((ny,)), dma((ny,)),
                dma((e,)), dma((e,)),
                dma((nz,)), dma((nz,)),
                dma((e,)), dma((e,)),
            ],
            compiler_params=pltpu.CompilerParams(
                collective_id=0, has_side_effects=True, vmem_limit_bytes=67043328
            ),
        )(plan, lengths, filters, query[0], key[0], value[0], out_grad[0], weight)
        moved = pl.pallas_call(
            hand_over,
            name="results",
            out_shape=[jax.ShapeDtypeStruct(o.shape, o.dtype) for o in outs],
            in_specs=[hbm] * 5,
            out_specs=[hbm] * 5,
            scratch_shapes=[pltpu.VMEM(o.shape, o.dtype) for o in outs] + [dma((5,)), dma((5,))],
        )(*outs)
        mixed, qg, kg, vg, fg = moved
        return mixed[None], qg[None], kg[None], vg[None], fg.reshape(groups, taps)

    rows = P(DP, CONTEXT, TP)
    split = P(TP, None)
    return jax.shard_map(
        per_device,
        mesh=finer,
        in_specs=(rows, rows, rows, split, split, P(DP, None), P(DP, None), rows),
        out_specs=(rows, rows, rows, rows, split),
        check_vma=False,
    )


def solution(mesh):
    return build(mesh, 4, mesh.shape["context"] // 4)
```

time: 95.2 us -> 73.5 us (0.77)
  Pallas kernels: 84.5 us -> 71.4 us
  local copies, waits for them, and re-layouts: 8.84 us -> 0 us
    pallas_call x1, Pallas kernels: 84.5 us -> 68.9 us  [per_device(): pl.pallas_call(functools.partial(layer_kernel, cfg), name='layer', out_sh...]
    unnamed x5 -> x0, local copies, waits for them, and re-layouts: 8.84 us -> none
    pallas_call x0 -> x1, Pallas kernels: none -> 2.44 us  [per_device(): pl.pallas_call(hand_over, name='results', out_shape=[jax.ShapeDtypeStruct...]
where the time goes in v2:
time: 73.5 us; the launch traced here: 72.2 us
  Pallas kernels  71.4 us (97%)
  between operations  0.8 us (1%)
    pallas_call x1, Pallas kernels, per_device(): pl.pallas_call(functools.partial(layer_kernel, cfg), name='layer', out_sh...  68.9 us
    pallas_call x1, Pallas kernels, per_device(): pl.pallas_call(hand_over, name='results', out_shape=[jax.ShapeDtypeStruct...  2.44 us

profile of v2, /device:TPU:8, one launch (start us, length us, event | category | flops | bytes accessed | tf_op | source)
XLA Modules:
  0.0 72.2 jit_solution(4606233932895538474)
XLA Ops:
  0.6 68.9 %layer.1 = (bf16[256,1024]{1,0:T(8,128)(2,1)}, bf16[256,1024]{1,0:T(8,128)(2,1)}, bf16[256,1024]{1,0:T(8,128)(2,1)}, bf16[256,1024]{1,0:T(8,128)(2,1)}, f32[8,8,128]{2,1,0:T(8,128)}) custom-call(s32[1,1024]{1,0:T(1,128)} %plan_hbm.1, s32[1,32]{1,0:T(1,128)} %len_hbm.1, bf16[64,128]{1,0:T(8,128)(2,1)} %filt_hbm.1, bf16[256,1024]{1,0:T(8,128)(2,1)} %bitcast.9, ...), custom_call_target="tpu_custom_call" | custom-call | tf_op jit(solution)/shard_map/layer/pallas_call | solution.py:554
  69.6 2.4 %results.1 = (bf16[256,1024]{1,0:T(8,128)(2,1)}, bf16[256,1024]{1,0:T(8,128)(2,1)}, bf16[256,1024]{1,0:T(8,128)(2,1)}, bf16[256,1024]{1,0:T(8,128)(2,1)}, f32[8,8,128]{2,1,0:T(8,128)}) custom-call(bf16[256,1024]{1,0:T(8,128)(2,1)} %get-tuple-element.15.refs_0_, bf16[256,1024]{1,0:T(8,128)(2,1)} %get-tuple-element.16.refs_1_, ...), custom_call_target="tpu_custom_call" | custom-call | tf_op jit(solution)/shard_map/results/pallas_call | solution.py:600

commit v3 on v2

--- a/solution.py
+++ b/solution.py
@@ -53,7 +53,7 @@
     plan_s, len_s, plan_v, filt_v, mixed_o, qg_o, kg_o, vg_o, fg_o,
     xp, xq, kv, vv, w, og, fmat, hmat, pmat, rmat, sbuf, rbuf, sbuf2, rbuf2,
     qo, pw, cbw, x2, gated, conv, gg, acc, tf, tb, mf, mb, mflip,
-    rs_send, rs_recv, tap, tap1, tap2, tap3,
+    rs_send, rs_mid, rs_fin, tap, tap1, tap2, tap3,
     small, out_sem, ld, fs, fr, ags, agr, phs, phr, chs, chr_, bs, br, rss, rsr, t1s, t1r, t2s, t2r, t3s, t3r,
 ):
     n, nx, nz, ny, ndp = cfg["n"], cfg["nx"], cfg["nz"], cfg["ny"], cfg["ndp"]
@@ -81,39 +81,42 @@
     def after(k):
         return lax.rem(me + k, n)
 
-    barrier = pltpu.get_barrier_semaphore()
-
-    @pl.loop(1, n)
-    def _(k):
-        pl.semaphore_signal(barrier, inc=1, device_id=ctx(after(k)), device_id_type=MESH_ID)
-
-    for k in range(1, ny):
-        pl.semaphore_signal(
-            barrier, inc=1, device_id={TP: lax.rem(ty + k, ny)}, device_id_type=MESH_ID
-        )
-    for d in range(1, ndp):
-        for k in range(nx):
-            to = {DP: lax.rem(dp + d, ndp), CX: lax.rem(cx + k, nx)}
-            pl.semaphore_signal(barrier, inc=1, device_id=to, device_id_type=MESH_ID)
-    greeted = (n - 1) + (ny - 1) + (ndp - 1) * nx
-
     moves = [(k_hbm, kv), (v_hbm, vv), (og_hbm, og.at[ty])]
     for h in range(HALVES):
         for p in range(2):
             moves.append((q_hbm.at[:, pl.ds(h * hw + p * uw, uw)], xq.at[h, pl.ds(p * length, length)]))
     moves.append((w_hbm, w))
     loads = [pltpu.make_async_copy(src, dst, ld.at[i]) for i, (src, dst) in enumerate(moves)]
+    small_moves = [(plan_hbm, plan_s), (plan_hbm, plan_v), (filt_hbm, filt_v), (len_hbm, len_s)]
     smalls = [
-        pltpu.make_async_copy(src, dst, small.at[i])
-        for i, (src, dst) in enumerate(
-            [(plan_hbm, plan_s), (plan_hbm, plan_v), (filt_hbm, filt_v), (len_hbm, len_s)]
-        )
+        pltpu.make_async_copy(src, dst, small.at[i]) for i, (src, dst) in enumerate(small_moves)
     ]
-    for load in smalls[:1] + loads[:2] + smalls[1:] + loads[2:]:
+    smalls[0].start()
+
+    barrier = pltpu.get_barrier_semaphore()
+
+    def greet(to):
+        pl.semaphore_signal(barrier, inc=1, device_id=to, device_id_type=MESH_ID)
+
+    def far_first(count):
+        return sorted(range(count), key=lambda d: -min(d, count - d))
+
+    for dx in far_first(nx):
+        for dz in far_first(nz):
+            if (dx, dz) != (0, 0):
+                greet({CX: lax.rem(cx + dx, nx), CZ: lax.rem(cz + dz, nz)})
+    for d in range(1, ndp):
+        for k in far_first(nx):
+            greet({DP: lax.rem(dp + d, ndp), CX: lax.rem(cx + k, nx)})
+    for k in range(1, ny):
+        greet({TP: lax.rem(ty + k, ny)})
+    greeted = (n - 1) + (ny - 1) + (ndp - 1) * nx
+    for load in loads[:2] + smalls[1:] + loads[2:]:
         load.start()
 
     smalls[0].wait()
 
+    sc = mark('fbuild'); sc.__enter__()
     b = iota((8, 2 * length), 1)
     panel = (b >> lgp) & (n - 1)
     owner = jnp.zeros((8, 2 * length), I32)
@@ -122,8 +125,10 @@
     target = owner * (2 * psz) + (b >> log2(length)) * psz + (b & (psz - 1))
     square = iota((2 * length, 2 * length), 0)
     fmat[...] = ones_where(square == target[0:1]).astype(BF)
-    for load in loads[:2]:
-        load.wait()
+    sc.__exit__(None, None, None)
+    with mark('kvwait'):
+        for load in loads[:2]:
+            load.wait()
 
     def to_blocks(value):
         return value.astype(BF).reshape(n, 2 * psz, uw)
@@ -134,9 +139,11 @@
             xp[h, p * length : (p + 1) * length] = (
                 kv[:, at].astype(F32) * vv[:, at].astype(F32)
             ).astype(BF)
-        sbuf[h] = to_blocks(mm(fmat[...], xp[h]))
-        rbuf[h, me] = sbuf[h, me]
-
+    def own_blocks(u, x):
+        sbuf[u] = to_blocks(mm(fmat[...], x))
+        rbuf[u, me] = sbuf[u, me]
+
+    own_blocks(0, xp[0])
     with mark("barrier"):
         pl.semaphore_wait(barrier, greeted)
 
@@ -175,6 +182,7 @@
         piece = og.at[source, part]
         return start(piece, piece, ags.at[i], agr.at[i], to)
 
+    send_forward(0)
     loads[2].wait()
     ag = [
         pass_on(ty, first, up, 0),
@@ -182,13 +190,12 @@
         pass_on(ty, second, up, 2),
         pass_on(ty, first, down, 3),
     ]
-    send_forward(0)
+    own_blocks(1, xp[1])
     send_forward(1)
     for h in range(HALVES):
         for load in loads[3 + 2 * h : 5 + 2 * h]:
             load.wait()
-        sbuf[HALVES + h] = to_blocks(mm(fmat[...], xq[h]))
-        rbuf[HALVES + h, me] = sbuf[HALVES + h, me]
+        own_blocks(HALVES + h, xq[h])
 
     for load in smalls[1:]:
         load.wait()
@@ -422,21 +429,33 @@
     receive_query(1)
     gate(1)
 
-    rs = []
-    with mark("proj"):
-        for k in range(1, ny):
-            to = lax.rem(ty + k, ny)
-            rs_send[k] = (acc[to] + project(to, 1)).astype(BF)
-            rs.append(start(rs_send.at[k], rs_recv.at[ty], rss.at[k], rsr.at[k], {TP: to}))
-        rs_recv[ty] = (acc[ty] + project(ty, 1)).astype(BF)
-
     filter_terms(1)
     firsts = []
-    for k in range(1, group_n):
-        to = lax.rem(e_me + k, group_n)
-        firsts.append(start(tap.at[to], tap1.at[e_me], t1s.at[k], t1r.at[k], peer_e(to)))
-    tap1[e_me] = tap[e_me]
+    for k in range(1, nz):
+        to = lax.rem(cz + k, nz)
+        firsts.append(start(tap.at[to], tap1.at[cz], t1s.at[k], t1r.at[k], {CZ: to}))
+    tap1[cz] = tap[cz]
     send_back(1)
+
+    lo, hi = slice(0, half), slice(half, length)
+
+    def reduce_send(i, dst, to):
+        return start(rs_send.at[i], dst, rss.at[i], rsr.at[i], to)
+
+    with mark("proj"):
+        part = acc[across] + project(across, 1)
+        rs_send[0] = part[lo].astype(BF)
+        rs_send[1] = part[hi].astype(BF)
+        rs = [reduce_send(0, rs_mid.at[0], up), reduce_send(1, rs_mid.at[1], down)]
+        part = acc[above] + project(above, 1)
+        rs_send[2] = part[hi].astype(BF)
+        rs.append(reduce_send(2, rs_fin.at[0], up))
+        acc[above, lo] = part[lo]
+        part = acc[below] + project(below, 1)
+        rs_send[3] = part[lo].astype(BF)
+        rs.append(reduce_send(3, rs_fin.at[1], down))
+        acc[below, hi] = part[hi]
+        acc[ty] = (acc[ty] + project(ty, 1)).astype(BF).astype(F32)
 
     product_back(0)
     send_back(2)
@@ -444,12 +463,19 @@
     with mark("t1wait"):
         for copy in firsts:
             copy.wait_recv()
-    tap2[cz] = jnp.sum(tap1[...], axis=0)
+    tap2[e_me] = jnp.sum(tap1[...], axis=0)
     seconds = []
-    for k in range(1, nz):
-        to = {CZ: lax.rem(cz + k, nz)}
-        seconds.append(start(tap2.at[cz], tap2.at[cz], t2s.at[k], t2r.at[k], to))
+    for k in range(1, group_n):
+        to = peer_e(lax.rem(e_me + k, group_n))
+        seconds.append(start(tap2.at[e_me], tap2.at[e_me], t2s.at[k], t2r.at[k], to))
     send_back(3)
+    with mark("rsmid"):
+        rs[0].wait_recv()
+        rs_send[4] = (acc[above, lo] + rs_mid[0].astype(F32)).astype(BF)
+        rs.append(reduce_send(4, rs_fin.at[2], up))
+        rs[1].wait_recv()
+        rs_send[5] = (acc[below, hi] + rs_mid[1].astype(F32)).astype(BF)
+        rs.append(reduce_send(5, rs_fin.at[3], down))
 
     leaving = []
 
@@ -476,36 +502,35 @@
             leave(held.at[:, at], out.at[:, at])
 
     loader_rows(0)
-    loader_rows(1)
     with mark("t2wait"):
         for copy in seconds:
             copy.wait_recv()
     summed = tap2[0]
-    for z in range(1, nz):
-        summed = summed + tap2[z]
+    for i in range(1, group_n):
+        summed = summed + tap2[i]
     scale = 1.0 / math.sqrt(float(ndp * total))
     mirror = ones_where(lane == taps - 1 - row)
-    fg_o[e_me] = scale * jnp.dot(
+    fg_o[cz] = scale * jnp.dot(
         summed, mirror, precision=lax.Precision.HIGHEST, preferred_element_type=F32
     )
     thirds = []
-    for k in range(1, group_n):
-        to = peer_e(lax.rem(e_me + k, group_n))
-        thirds.append(start(fg_o.at[e_me], fg_o.at[e_me], t3s.at[k], t3r.at[k], to))
+    for k in range(1, nz):
+        to = {CZ: lax.rem(cz + k, nz)}
+        thirds.append(start(fg_o.at[cz], fg_o.at[cz], t3s.at[k], t3r.at[k], to))
+    loader_rows(1)
     loader_rows(2)
     with mark("rswait"):
-        for copy in rs:
+        for copy in rs[2:]:
             copy.wait_recv()
-    summed = rs_recv[0].astype(F32)
-    for y in range(1, ny):
-        summed = summed + rs_recv[y].astype(F32)
-    mixed_o[...] = summed.astype(BF)
+    for rows_of, one, two in ((lo, 1, 2), (hi, 0, 3)):
+        summed = acc[ty, rows_of] + rs_fin[one].astype(F32) + rs_fin[two].astype(F32)
+        mixed_o[rows_of] = summed.astype(BF)
     leave(mixed_o, mixed_h)
+    loader_rows(3)
     with mark("t3wait"):
         for copy in thirds:
             copy.wait_recv()
     leave(fg_o, fg_h)
-    loader_rows(3)
 
     with mark("drain"):
         for copy in ag + rs + prod_halo + back_halo + firsts + seconds + thirds:
@@ -521,8 +546,14 @@
     count = (len(refs) - 2) // 3
     srcs, dsts, held = refs[:count], refs[count : 2 * count], refs[2 * count : 3 * count]
     sem_in, sem_out = refs[3 * count :]
-    ins = [pltpu.make_async_copy(a, b, sem_in.at[i]) for i, (a, b) in enumerate(zip(srcs, held, strict=True))]
-    outs = [pltpu.make_async_copy(b, a, sem_out.at[i]) for i, (a, b) in enumerate(zip(dsts, held, strict=True))]
+    ins, outs = [], []
+    for a, b, c in zip(srcs, held, dsts, strict=True):
+        pieces = 1
+        rows = a.shape[0] // pieces
+        for p in range(pieces):
+            at, i = pl.ds(p * rows, rows), len(ins)
+            ins.append(pltpu.make_async_copy(a.at[at], b.at[at], sem_in.at[i]))
+            outs.append(pltpu.make_async_copy(b.at[at], c.at[at], sem_out.at[i]))
     for copy in ins:
         copy.start()
     for arrive, leave in zip(ins, outs, strict=True):
@@ -550,11 +581,11 @@
         dma = pltpu.SemaphoreType.DMA
         row = jax.ShapeDtypeStruct((length, width), BF)
         e = ndp * nx
-        assert groups == e * 8
+        assert groups == nz * 8
         outs = pl.pallas_call(
             functools.partial(layer_kernel, cfg),
             name="layer",
-            out_shape=[row, row, row, row, jax.ShapeDtypeStruct((e, 8, taps), F32)],
+            out_shape=[row, row, row, row, jax.ShapeDtypeStruct((nz, 8, taps), F32)],
             in_specs=[hbm] * 8,
             out_specs=[hbm] * 5,
             scratch_shapes=[
@@ -563,7 +594,7 @@
                 pltpu.VMEM(plan.shape, I32),
                 pltpu.VMEM(filters.shape, BF),
                 *[pltpu.VMEM((length, width), BF)] * 4,
-                pltpu.VMEM((e, 8, taps), F32),
+                pltpu.VMEM((nz, 8, taps), F32),
                 *[pltpu.VMEM((HALVES, 2 * length, uw), BF)] * 2,
                 pltpu.VMEM((length, width), BF),
                 pltpu.VMEM((length, width), BF),
@@ -579,19 +610,19 @@
                 pltpu.VMEM((ny, length, width), F32),
                 *[pltpu.VMEM((blocks, groups * taps, 2 * taps), BF)] * 2,
                 *[pltpu.VMEM((blocks, taps, 2 * taps), F32)] * 3,
-                *[pltpu.VMEM((ny, length, width), BF)] * 2,
-                *[pltpu.VMEM((e, 8, taps), F32)] * 2,
-                pltpu.VMEM((nz, 8, taps), F32),
+                *[pltpu.VMEM((k, length // 2, width), BF) for k in (6, 2, 4)],
+                *[pltpu.VMEM((nz, 8, taps), F32)] * 2,
+                pltpu.VMEM((e, 8, taps), F32),
                 pltpu.VMEM((2, groups, taps), F32),
                 dma((4,)), dma((8,)), dma((8,)),
                 dma((UNITS,)), dma((UNITS,)),
                 dma((6,)), dma((6,)),
                 *[dma((HALVES,))] * 4,
                 dma((UNITS,)), dma((UNITS,)),
-                dma((ny,)), dma((ny,)),
+                dma((6,)), dma((6,)),
+                dma((nz,)), dma((nz,)),
                 dma((e,)), dma((e,)),
                 dma((nz,)), dma((nz,)),
-                dma((e,)), dma((e,)),
             ],
             compiler_params=pltpu.CompilerParams(
                 collective_id=0, has_side_effects=True, vmem_limit_bytes=67043328
@@ -603,7 +634,7 @@
             out_shape=[jax.ShapeDtypeStruct(o.shape, o.dtype) for o in outs],
             in_specs=[hbm] * 5,
             out_specs=[hbm] * 5,
-            scratch_shapes=[pltpu.VMEM(o.shape, o.dtype) for o in outs] + [dma((5,)), dma((5,))],
+            scratch_shapes=[pltpu.VMEM(o.shape, o.dtype) for o in outs] + [dma((17,)), dma((17,))],
         )(*outs)
         mixed, qg, kg, vg, fg = moved
         return mixed[None], qg[None], kg[None], vg[None], fg.reshape(groups, taps)

time: 73.5 us -> 70.2 us (0.955); the launches traced: 72.2 us -> 70 us
  Pallas kernels: 71.4 us -> 69.2 us
    pallas_call x1, Pallas kernels: 68.9 us -> 66.5 us  [per_device(): pl.pallas_call(functools.partial(layer_kernel, cfg), name='layer', out_sh...]
where the time goes in v3:
time: 70.2 us; the launch traced here: 70 us
  Pallas kernels  69.2 us (99%)
  between operations  0.8 us (1%)
    pallas_call x1, Pallas kernels, per_device(): pl.pallas_call(functools.partial(layer_kernel, cfg), name='layer', out_sh...  66.5 us
    pallas_call x1, Pallas kernels, per_device(): pl.pallas_call(hand_over, name='results', out_shape=[jax.ShapeDtypeStruct...  2.66 us

profile of v3, /device:TPU:8, one launch (start us, length us, event | category | flops | bytes accessed | tf_op | source)
XLA Modules:
  0.0 70.0 jit_solution(17475616759996359445)
XLA Ops:
  0.6 66.5 %layer.1 = (bf16[256,1024]{1,0:T(8,128)(2,1)}, bf16[256,1024]{1,0:T(8,128)(2,1)}, bf16[256,1024]{1,0:T(8,128)(2,1)}, bf16[256,1024]{1,0:T(8,128)(2,1)}, f32[8,8,128]{2,1,0:T(8,128)}) custom-call(s32[1,1024]{1,0:T(1,128)} %plan_hbm.1, s32[1,32]{1,0:T(1,128)} %len_hbm.1, bf16[64,128]{1,0:T(8,128)(2,1)} %filt_hbm.1, bf16[256,1024]{1,0:T(8,128)(2,1)} %bitcast.9, ...), custom_call_target="tpu_custom_call" | custom-call | tf_op jit(solution)/shard_map/layer/pallas_call | solution.py:585
  67.2 2.7 %results.1 = (bf16[256,1024]{1,0:T(8,128)(2,1)}, bf16[256,1024]{1,0:T(8,128)(2,1)}, bf16[256,1024]{1,0:T(8,128)(2,1)}, bf16[256,1024]{1,0:T(8,128)(2,1)}, f32[8,8,128]{2,1,0:T(8,128)}) custom-call(bf16[256,1024]{1,0:T(8,128)(2,1)} %get-tuple-element.15.refs_0_, bf16[256,1024]{1,0:T(8,128)(2,1)} %get-tuple-element.16.refs_1_, ...), custom_call_target="tpu_custom_call" | custom-call | tf_op jit(solution)/shard_map/results/pallas_call | solution.py:631

commit v4 on v3

--- a/solution.py
+++ b/solution.py
@@ -54,7 +54,7 @@
     xp, xq, kv, vv, w, og, fmat, hmat, pmat, rmat, sbuf, rbuf, sbuf2, rbuf2,
     qo, pw, cbw, x2, gated, conv, gg, acc, tf, tb, mf, mb, mflip,
     rs_send, rs_mid, rs_fin, tap, tap1, tap2, tap3,
-    small, out_sem, ld, fs, fr, ags, agr, phs, phr, chs, chr_, bs, br, rss, rsr, t1s, t1r, t2s, t2r, t3s, t3r,
+    small, out_sem, ld, fs, fr, ags, agr, phs, phr, chs, chr_, bs, br, rss, rsr, ts,
 ):
     n, nx, nz, ny, ndp = cfg["n"], cfg["nx"], cfg["nz"], cfg["ny"], cfg["ndp"]
     length, width, taps, docs = cfg["length"], cfg["width"], cfg["taps"], cfg["docs"]
@@ -160,14 +160,17 @@
         return copy
 
     def send_blocks(src, dst, ssem, rsem):
-        @pl.loop(1, n)
+        @pl.loop(0, n - 1)
         def _(k):
-            to = after(k)
-            start(src.at[to], dst.at[me], ssem, rsem, ctx(to))
+            px, pz = lax.rem(k, nx), k // nx
+            dx = nx // 2 + ((px + 1) // 2) * (1 - 2 * lax.rem(px, 2))
+            dz = nz // 2 + ((pz + 1) // 2) * (1 - 2 * lax.rem(pz, 2))
+            x, z = lax.rem(cx + dx, nx), lax.rem(cz + dz, nz)
+            start(src.at[x * nz + z], dst.at[me], ssem, rsem, {CX: x, CZ: z})
 
     def send_forward(u):
         with mark("send"):
-            send_blocks(sbuf.at[u], rbuf.at[u], fs.at[u], fr.at[u])
+            send_blocks(sbuf.at[u], rbuf.at[u], fs, fr.at[u])
 
     def wait_bytes(ref, sem):
         pltpu.make_async_copy(ref, ref, sem).wait()
@@ -363,7 +366,7 @@
 
     def send_back(u):
         with mark("send2"):
-            send_blocks(sbuf2.at[u], rbuf2.at[u], bs.at[u], br.at[u])
+            send_blocks(sbuf2.at[u], rbuf2.at[u], bs, br.at[u])
 
     def filter_terms(h):
         with mark("terms"):
@@ -389,6 +392,9 @@
                     )
 
     circulants(tf, mf, 1)
+    with mark("wwait"):
+        loads[-1].wait()
+    add_grad(ty, True)
     receive_product(0)
     with mark("agw"):
         ag[0].wait_recv()
@@ -398,17 +404,14 @@
     eye = ones_where(square == iota((2 * length, 2 * length), 1)).astype(BF)
     rmat[...] = mm_nt(eye, pmat[...]).astype(BF)
     hmat[...] = mm_nt(eye, fmat[...]).astype(BF)
-    with mark("wwait"):
-        loads[-1].wait()
-    add_grad(ty, True)
+    circulants(tb, mb, 0)
     receive_product(1)
-    circulants(tb, mb, 0)
-    filter_forward(0)
     with mark("agw2"):
         ag[2].wait_recv()
         ag[3].wait_recv()
     add_grad(below, False)
     add_grad(above, False)
+    filter_forward(0)
     with mark("agw3"):
         ag[4].wait_recv()
         ag[5].wait_recv()
@@ -430,10 +433,9 @@
     gate(1)
 
     filter_terms(1)
-    firsts = []
     for k in range(1, nz):
         to = lax.rem(cz + k, nz)
-        firsts.append(start(tap.at[to], tap1.at[cz], t1s.at[k], t1r.at[k], {CZ: to}))
+        start(tap.at[to], tap1.at[cz], ts.at[0], ts.at[1], {CZ: to})
     tap1[cz] = tap[cz]
     send_back(1)
 
@@ -461,13 +463,11 @@
     send_back(2)
     product_back(1)
     with mark("t1wait"):
-        for copy in firsts:
-            copy.wait_recv()
+        wait_bytes(tap1.at[pl.ds(0, nz - 1)], ts.at[1])
     tap2[e_me] = jnp.sum(tap1[...], axis=0)
-    seconds = []
     for k in range(1, group_n):
         to = peer_e(lax.rem(e_me + k, group_n))
-        seconds.append(start(tap2.at[e_me], tap2.at[e_me], t2s.at[k], t2r.at[k], to))
+        start(tap2.at[e_me], tap2.at[e_me], ts.at[2], ts.at[3], to)
     send_back(3)
     with mark("rsmid"):
         rs[0].wait_recv()
@@ -503,8 +503,7 @@
 
     loader_rows(0)
     with mark("t2wait"):
-        for copy in seconds:
-            copy.wait_recv()
+        wait_bytes(tap2.at[pl.ds(0, group_n - 1)], ts.at[3])
     summed = tap2[0]
     for i in range(1, group_n):
         summed = summed + tap2[i]
@@ -513,10 +512,9 @@
     fg_o[cz] = scale * jnp.dot(
         summed, mirror, precision=lax.Precision.HIGHEST, preferred_element_type=F32
     )
-    thirds = []
     for k in range(1, nz):
         to = {CZ: lax.rem(cz + k, nz)}
-        thirds.append(start(fg_o.at[cz], fg_o.at[cz], t3s.at[k], t3r.at[k], to))
+        start(fg_o.at[cz], fg_o.at[cz], ts.at[4], ts.at[5], to)
     loader_rows(1)
     loader_rows(2)
     with mark("rswait"):
@@ -528,16 +526,17 @@
     leave(mixed_o, mixed_h)
     loader_rows(3)
     with mark("t3wait"):
-        for copy in thirds:
-            copy.wait_recv()
+        wait_bytes(fg_o.at[pl.ds(0, nz - 1)], ts.at[5])
     leave(fg_o, fg_h)
 
     with mark("drain"):
-        for copy in ag + rs + prod_halo + back_halo + firsts + seconds + thirds:
+        for copy in ag + rs + prod_halo + back_halo:
             copy.wait_send()
-        for u in range(UNITS):
-            wait_bytes(sbuf.at[u, pl.ds(0, n - 1)], fs.at[u])
-            wait_bytes(sbuf2.at[u, pl.ds(0, n - 1)], bs.at[u])
+        wait_bytes(tap1.at[pl.ds(0, nz - 1)], ts.at[0])
+        wait_bytes(tap2.at[pl.ds(0, group_n - 1)], ts.at[2])
+        wait_bytes(fg_o.at[pl.ds(0, nz - 1)], ts.at[4])
+        wait_bytes(sbuf.at[:, pl.ds(0, n - 1)], fs)
+        wait_bytes(sbuf2.at[:, pl.ds(0, n - 1)], bs)
         for copy in leaving:
             copy.wait()
 
@@ -615,14 +614,12 @@
                 pltpu.VMEM((e, 8, taps), F32),
                 pltpu.VMEM((2, groups, taps), F32),
                 dma((4,)), dma((8,)), dma((8,)),
-                dma((UNITS,)), dma((UNITS,)),
+                dma, dma((UNITS,)),
                 dma((6,)), dma((6,)),
                 *[dma((HALVES,))] * 4,
-                dma((UNITS,)), dma((UNITS,)),
+                dma, dma((UNITS,)),
                 dma((6,)), dma((6,)),
-                dma((nz,)), dma((nz,)),
-                dma((e,)), dma((e,)),
-                dma((nz,)), dma((nz,)),
+                dma((6,)),
             ],
             compiler_params=pltpu.CompilerParams(
                 collective_id=0, has_side_effects=True, vmem_limit_bytes=67043328
@@ -634,7 +631,7 @@
             out_shape=[jax.ShapeDtypeStruct(o.shape, o.dtype) for o in outs],
             in_specs=[hbm] * 5,
             out_specs=[hbm] * 5,
-            scratch_shapes=[pltpu.VMEM(o.shape, o.dtype) for o in outs] + [dma((17,)), dma((17,))],
+            scratch_shapes=[pltpu.VMEM(o.shape, o.dtype) for o in outs] + [dma((5,)), dma((5,))],
         )(*outs)
         mixed, qg, kg, vg, fg = moved
         return mixed[None], qg[None], kg[None], vg[None], fg.reshape(groups, taps)

time: 70.2 us -> 69.1 us (0.984)
  Pallas kernels: 69.2 us -> 68.2 us
    pallas_call x1, Pallas kernels: 66.5 us -> 65.8 us  [per_device(): pl.pallas_call(functools.partial(layer_kernel, cfg), name='layer', out_sh...]
where the time goes in v4:
time: 69.1 us; the launch traced here: 69 us
  Pallas kernels  68.2 us (99%)
  between operations  0.8 us (1%)
    pallas_call x1, Pallas kernels, per_device(): pl.pallas_call(functools.partial(layer_kernel, cfg), name='layer', out_sh...  65.8 us
    pallas_call x1, Pallas kernels, per_device(): pl.pallas_call(hand_over, name='results', out_shape=[jax.ShapeDtypeStruct...  2.44 us

profile of v4, /device:TPU:8, one launch (start us, length us, event | category | flops | bytes accessed | tf_op | source)
XLA Modules:
  0.0 69.0 jit_solution(15186526841967721503)
XLA Ops:
  0.6 65.8 %layer.1 = (bf16[256,1024]{1,0:T(8,128)(2,1)}, bf16[256,1024]{1,0:T(8,128)(2,1)}, bf16[256,1024]{1,0:T(8,128)(2,1)}, bf16[256,1024]{1,0:T(8,128)(2,1)}, f32[8,8,128]{2,1,0:T(8,128)}) custom-call(s32[1,1024]{1,0:T(1,128)} %plan_hbm.1, s32[1,32]{1,0:T(1,128)} %len_hbm.1, bf16[64,128]{1,0:T(8,128)(2,1)} %filt_hbm.1, bf16[256,1024]{1,0:T(8,128)(2,1)} %bitcast.9, ...), custom_call_target="tpu_custom_call" | custom-call | tf_op jit(solution)/shard_map/layer/pallas_call | solution.py:584
  66.4 2.4 %results.1 = (bf16[256,1024]{1,0:T(8,128)(2,1)}, bf16[256,1024]{1,0:T(8,128)(2,1)}, bf16[256,1024]{1,0:T(8,128)(2,1)}, bf16[256,1024]{1,0:T(8,128)(2,1)}, f32[8,8,128]{2,1,0:T(8,128)}) custom-call(bf16[256,1024]{1,0:T(8,128)(2,1)} %get-tuple-element.15.refs_0_, bf16[256,1024]{1,0:T(8,128)(2,1)} %get-tuple-element.16.refs_1_, ...), custom_call_target="tpu_custom_call" | custom-call | tf_op jit(solution)/shard_map/results/pallas_call | solution.py:628

commit v5 on v4

--- a/solution.py
+++ b/solution.py
@@ -432,6 +432,17 @@
     receive_query(1)
     gate(1)
 
+    lo, hi = slice(0, half), slice(half, length)
+
+    def reduce_send(i, dst, to):
+        return start(rs_send.at[i], dst, rss.at[i], rsr.at[i], to)
+
+    with mark("across"):
+        part = acc[across] + project(across, 1)
+        rs_send[0] = part[lo].astype(BF)
+        rs_send[1] = part[hi].astype(BF)
+        rs = [reduce_send(0, rs_mid.at[0], up), reduce_send(1, rs_mid.at[1], down)]
+
     filter_terms(1)
     for k in range(1, nz):
         to = lax.rem(cz + k, nz)
@@ -439,16 +450,7 @@
     tap1[cz] = tap[cz]
     send_back(1)
 
-    lo, hi = slice(0, half), slice(half, length)
-
-    def reduce_send(i, dst, to):
-        return start(rs_send.at[i], dst, rss.at[i], rsr.at[i], to)
-
     with mark("proj"):
-        part = acc[across] + project(across, 1)
-        rs_send[0] = part[lo].astype(BF)
-        rs_send[1] = part[hi].astype(BF)
-        rs = [reduce_send(0, rs_mid.at[0], up), reduce_send(1, rs_mid.at[1], down)]
         part = acc[above] + project(above, 1)
         rs_send[2] = part[hi].astype(BF)
         rs.append(reduce_send(2, rs_fin.at[0], up))
@@ -496,10 +498,15 @@
                 qg_o[:, at] = part.astype(BF)
             else:
                 kg_o[:, at] = (part * vv[:, at].astype(F32)).astype(BF)
+        half_at = pl.ds(h * hw, hw)
+        held, out = (qg_o, qg_h) if u < HALVES else (kg_o, kg_h)
+        leave(held.at[:, half_at], out.at[:, half_at])
+        if u >= HALVES:
+            for p in range(2):
+                part = home[p * length : (p + 1) * length]
+                at = slice(h * hw + p * uw, h * hw + (p + 1) * uw)
                 vg_o[:, at] = (part * kv[:, at].astype(F32)).astype(BF)
-        at = pl.ds(h * hw, hw)
-        for held, out in [(qg_o, qg_h)] if u < HALVES else [(kg_o, kg_h), (vg_o, vg_h)]:
-            leave(held.at[:, at], out.at[:, at])
+            leave(vg_o.at[:, half_at], vg_h.at[:, half_at])
 
     loader_rows(0)
     with mark("t2wait"):

time: 69.1 us -> 69.4 us (level)
  no operation moved by 1% of the time
where the time goes in v5:
time: 69.4 us; the launch traced here: 69.3 us
  Pallas kernels  68.5 us (99%)
  between operations  0.8 us (1%)
    pallas_call x1, Pallas kernels, per_device(): pl.pallas_call(functools.partial(layer_kernel, cfg), name='layer', out_sh...  66.1 us
    pallas_call x1, Pallas kernels, per_device(): pl.pallas_call(hand_over, name='results', out_shape=[jax.ShapeDtypeStruct...  2.44 us

profile of v5, /device:TPU:8, one launch (start us, length us, event | category | flops | bytes accessed | tf_op | source)
XLA Modules:
  0.0 69.3 jit_solution(4659290122129448170)
XLA Ops:
  0.6 66.1 %layer.1 = (bf16[256,1024]{1,0:T(8,128)(2,1)}, bf16[256,1024]{1,0:T(8,128)(2,1)}, bf16[256,1024]{1,0:T(8,128)(2,1)}, bf16[256,1024]{1,0:T(8,128)(2,1)}, f32[8,8,128]{2,1,0:T(8,128)}) custom-call(s32[1,1024]{1,0:T(1,128)} %plan_hbm.1, s32[1,32]{1,0:T(1,128)} %len_hbm.1, bf16[64,128]{1,0:T(8,128)(2,1)} %filt_hbm.1, bf16[256,1024]{1,0:T(8,128)(2,1)} %bitcast.9, ...), custom_call_target="tpu_custom_call" | custom-call | tf_op jit(solution)/shard_map/layer/pallas_call | solution.py:591
  66.7 2.4 %results.1 = (bf16[256,1024]{1,0:T(8,128)(2,1)}, bf16[256,1024]{1,0:T(8,128)(2,1)}, bf16[256,1024]{1,0:T(8,128)(2,1)}, bf16[256,1024]{1,0:T(8,128)(2,1)}, f32[8,8,128]{2,1,0:T(8,128)}) custom-call(bf16[256,1024]{1,0:T(8,128)(2,1)} %get-tuple-element.15.refs_0_, bf16[256,1024]{1,0:T(8,128)(2,1)} %get-tuple-element.16.refs_1_, ...), custom_call_target="tpu_custom_call" | custom-call | tf_op jit(solution)/shard_map/results/pallas_call | solution.py:635
